TPU v7x, 256 devices: a whole 4x4x8 slice. The times are simulated.
256 devices in a mesh: samp: 4 (over z_hi, core), vert: 64 (over x, z_lo, y).
Axes of the slice: x: 4, y: 4, z: 8 (z_hi: 2, z_lo: 4; z = z_hi * 4 + z_lo), core: 2. Of those that a mesh axis runs over, the one named last changes fastest.
Arguments:
- inputs: bfloat16 [8, 262144, 128], P('samp', 'vert'), may hold values from -6 to 6
- cotangent: bfloat16 [8, 262144, 128], P('samp', 'vert'), may hold values from -6 to 6
- basis: bfloat16 [262144, 1024], P('vert'), may hold values from -0.0234375 to 0.0234375
- mode_weights: bfloat16 [1024, 128, 128], P('vert'), may hold values from -0.5 to 0.5
- w_up: bfloat16 [128, 512], replicated, may hold values from -0.5 to 0.5
- b_up: float32 [512], replicated, may hold values from -4 to 4
- w_down: bfloat16 [512, 128], replicated, may hold values from -0.25 to 0.25
Outputs:
- grad_input: bfloat16 [8, 262144, 128], P('samp', 'vert')
- grad_modes: float32 [1024, 128, 128], P('vert')
- grad_w_up: float32 [128, 512], replicated
- grad_b_up: float32 [512], replicated
- grad_w_down: float32 [512, 128], replicated
All inputs are finite; a program needn't handle non-finite values.
Results may differ from a plain program's by a relative error of at most 0.0055.
Values may be sent and summed in bfloat16 or wider, within the bound.
No kernel may reach another device: no remote copies, remote signals or barrier semaphores. Data moves between devices by JAX's collectives and lax.ppermute only.
A program may use at most 128 MiB of HBM per device.

v0:
```python
import jax
import jax.numpy as jnp
from jax import lax
from jax.sharding import PartitionSpec as P


def gelu_value(pre_act):
    inner = 0.7978845608 * (pre_act + 0.044715 * pre_act * pre_act * pre_act)
    return 0.5 * pre_act * (1.0 + jnp.tanh(inner))


def gelu_slope(pre_act):
    inner = 0.7978845608 * (pre_act + 0.044715 * pre_act * pre_act * pre_act)
    tangent = jnp.tanh(inner)
    return 0.5 * (1.0 + tangent) + 0.5 * pre_act * (1.0 - tangent * tangent) * 0.7978845608 * (
        1.0 + 3.0 * 0.044715 * pre_act * pre_act
    )


def spectral_part(grad_out, mode_weights, basis):
    mixing = mode_weights.astype(jnp.float32)
    grad_coef = jnp.einsum(
        "skd,kcd->skc", grad_out, mixing, precision=lax.Precision.HIGHEST
    ).astype(jnp.bfloat16)
    return jnp.einsum(
        "vk,skc->svc",
        basis,
        lax.all_gather(grad_coef, "vert", axis=1, tiled=True),
        preferred_element_type=jnp.float32,
    )


def pointwise_part(inputs, cotangent, w_up, b_up, w_down):
    samples_here = inputs.shape[0]
    vertices_here = inputs.shape[1]
    channels = inputs.shape[2]
    flat_inputs = inputs.reshape(samples_here * vertices_here, channels)
    flat_cotangent = cotangent.reshape(samples_here * vertices_here, channels)
    pre_act = jnp.dot(flat_inputs, w_up, preferred_element_type=jnp.float32) + b_up
    hidden = gelu_value(pre_act).astype(jnp.bfloat16)
    grad_hidden = jnp.dot(flat_cotangent, w_down.T, preferred_element_type=jnp.float32)
    grad_pre = (grad_hidden * gelu_slope(pre_act)).astype(jnp.bfloat16)
    pointwise = jnp.dot(grad_pre, w_up.T, preferred_element_type=jnp.float32)
    local_up = jnp.dot(flat_inputs.T, grad_pre, preferred_element_type=jnp.float32)
    local_bias = jnp.sum(grad_pre.astype(jnp.float32), axis=0)
    local_down = jnp.dot(hidden.T, flat_cotangent, preferred_element_type=jnp.float32)
    sums = lax.psum((local_up, local_bias, local_down), ("samp", "vert"))
    return (pointwise.reshape(samples_here, vertices_here, channels), sums)


def per_device(inputs, cotangent, basis, mode_weights, w_up, b_up, w_down):
    channels = inputs.shape[2]
    stacked = jnp.concatenate([inputs, cotangent], axis=2)
    projected = jnp.einsum("vk,svc->skc", basis, stacked, preferred_element_type=jnp.float32)
    owned_sums = lax.psum_scatter(projected, "vert", scatter_dimension=1, tiled=True)
    coeffs = owned_sums[:, :, :channels]
    grad_out = owned_sums[:, :, channels:]
    spectral = spectral_part(grad_out, mode_weights, basis)
    pointwise, mlp_grads = pointwise_part(inputs, cotangent, w_up, b_up, w_down)
    local_modes = jnp.einsum("skc,skd->kcd", coeffs, grad_out, precision=lax.Precision.HIGHEST)
    grad_modes = lax.psum(local_modes, "samp")
    grad_input = (spectral + pointwise).astype(jnp.bfloat16)
    grad_w_up, grad_b_up, grad_w_down = mlp_grads
    return (grad_input, grad_modes, grad_w_up, grad_b_up, grad_w_down)


def solution(mesh):
    in_specs = (
        P("samp", "vert", None),
        P("samp", "vert", None),
        P("vert", None),
        P("vert", None, None),
        P(),
        P(),
        P(),
    )
    out_specs = (P("samp", "vert", None), P("vert", None, None), P(), P(), P())
    return jax.shard_map(
        per_device, mesh=mesh, in_specs=in_specs, out_specs=out_specs, check_vma=False
    )
```

profile of v0, /device:TPU:0, one launch (start us, length us, event | category | flops | bytes accessed | tf_op | source)
XLA Modules:
  0.0 1230.6 jit_solution(3378659776492930055)
XLA Ops:
  7.2 0.0 copy-start
  7.2 0.0 all-reduce.10.cloned.1.call-start
  7.2 0.0 copy-start.2
  7.2 0.0 copy-start.6
  7.2 4.1 fusion.42
  11.3 0.0 copy-done.2
  11.3 0.0 copy-done.6
  11.3 0.0 copy-start.5
  11.4 7.7 fusion.11
  19.1 0.0 copy-done.5
  19.1 0.0 copy-start.1
  19.1 15.0 %convert_reduce_fusion = (f32[512]{0:T(512)S(1)}, bf16[8192,512]{1,0:T(8,128)(2,1)}) fusion(f32[8192,512]{1,0:T(8,128)S(1)} %fusion.42, f32[512]{0:T(512)S(1)} %copy-done.6, bf16[8192,128]{1,0:T(8,128)(2,1)} %bitcast.42, bf16[512,128]{1,0:T(8,128)(2,1)S(1)} %copy-done.5), kind=kOutput, calls=%fused_computation.10 | convolution fusion | flops 1166016000 | bytes 27398144 | tf_op jit(solution)/shard_map/dot_general | solution.py:41
  34.1 0.0 copy-done.1
  34.1 6.4 convolution_bitcast_fusion
  40.5 0.0 all-reduce.10.cloned.1.call-update
  40.6 0.2 all-reduce.8.cloned.1.call-start
  40.8 2.8 copy.32
  43.6 4.1 copy.33
  47.7 0.0 copy-start.3
  47.7 8.2 fusion.24
  55.9 2.3 copy.34
  58.2 0.0 all-reduce.8.cloned.1.call-update
  58.2 0.0 all-reduce.6.cloned.1.call-start
  58.3 0.0 copy-done.3
  58.3 7.7 fusion.43
  66.0 0.0 copy-start.7
  66.0 5.7 copy.36
  71.7 0.0 copy-done.7
  71.7 0.6 dynamic-slice
  72.9 79.6 %psum.30 = f32[512]{0:T(512)} all-reduce(f32[512]{0:T(512)S(1)} %get-tuple-element.27), channel_id=1, replica_groups=mesh['samp'=4,'vert'=64] {'samp','vert'}, use_global_device_ids=true, to_apply=%region_4.0 | all-reduce | flops 512 | bytes 4096 | tf_op jit(solution)/shard_map/psum | solution.py:47
  152.5 142.1 %all-reduce.10.cloned.1.call-done = (f32[128,512]{0,1:T(8,128)}, f32[512,128]{1,0:T(8,128)}) async-done(((f32[128,512]{0,1:T(8,128)}, f32[512,128]{1,0:T(8,128)}), (f32[128,512]{0,1:T(8,128)}, f32[512,128]{1,0:T(8,128)})) %all-reduce.10.cloned.1.call-update) | async-done | bytes 524304 | tf_op jit(solution)/shard_map/psum | solution.py:47
  294.5 1.8 copy.38
  296.3 717.1 %all-reduce.8.cloned.1.call-done = f32[2,1024,256]{2,0,1:T(2,128)} async-done(((f32[2,1024,256]{2,0,1:T(2,128)}), f32[2,1024,256]{2,0,1:T(2,128)}) %all-reduce.8.cloned.1.call-update) | async-done | bytes 2097168
  1013.5 3.5 fusion.31
  1017.0 0.0 all-reduce.6.cloned.1.call-update
  1017.0 0.0 copy-done
  1017.0 1.7 fusion.29
  1018.7 192.9 %all_gather.3 = bf16[2,1024,128]{2,0,1:T(2,128)(2,1)S(1)} all-gather(bf16[2,16,128]{2,0,1:T(2,128)(2,1)S(1)} %fusion.29), channel_id=1, replica_groups=mesh['samp'=4,'vert'=64] {'vert'}, dimensions={1}, use_global_device_ids=true | all-gather | bytes 532480 | tf_op jit(solution)/shard_map/all_gather | solution.py:28
  1211.6 0.0 copy-start.4
  1211.6 7.0 fusion.18
  1218.6 2.5 copy.37
  1221.1 0.0 all-reduce.6.cloned.1.call-done
  1221.1 2.3 copy.45
  1223.4 0.0 copy-done.4
  1223.4 0.7 copy.46
Async XLA Ops:
  7.2 1009.9 %copy-start = (bf16[16,128,128]{2,1,0:T(8,128)(2,1)S(1)}, bf16[16,128,128]{2,1,0:T(8,128)(2,1)}, u32[]{:S(2)}) copy-start(bf16[16,128,128]{2,1,0:T(8,128)(2,1)} %param.10) | copy-start | bytes 1572868
  7.2 287.4 %all-reduce.10.cloned.1.call-start = ((), (), s32[]{:S(2)}) async-start(), calls=%async_computation.2 | async-start | bytes 1048576 | tf_op jit(solution)/shard_map/psum | solution.py:47
  7.2 4.1 copy-start.2
  7.2 4.1 copy-start.6
  11.3 7.7 copy-start.5
  19.1 15.0 %copy-start.1 = (bf16[2,4096,128]{2,1,0:T(8,128)(2,1)S(1)}, bf16[2,4096,128]{2,1,0:T(8,128)(2,1)}, u32[]{:S(2)}) copy-start(bf16[2,4096,128]{2,1,0:T(8,128)(2,1)} %param.7) | copy-start | bytes 6291460
  40.6 972.9 %all-reduce.8.cloned.1.call-start = ((), (), s32[]{:S(2)}) async-start(), calls=%async_computation.1 | async-start | bytes 4194304
  47.7 10.6 copy-start.3
  58.2 1162.9 %all-reduce.6.cloned.1.call-start = ((), (), s32[]{:S(2)}) async-start(), calls=%async_computation | async-start | bytes 2097152 | tf_op jit(solution)/shard_map/psum | solution.py:61
  66.0 5.7 copy-start.7
  1211.6 11.8 copy-start.4
Sparse Core Ops, SparseCore 0:
  40.7 253.8 all-reduce.9
  297.7 715.6 all-reduce.7
  1017.1 68.9 all-reduce.5
where the time goes:
time: 1230 us
  waiting for transfers between devices  859 us (70%)
  blocking collectives  272 us (22%)
  matrix products  61.4 us (5%)
  local copies, waits for them, and re-layouts  22.7 us (2%)
  between operations  14.5 us (1%)
    unnamed x4, waiting for transfers between devices  717 us
    all_gather x1, blocking collectives, spectral_part(): lax.all_gather(grad_coef, 'vert', axis=1, tiled=True)  193 us
    psum x1, waiting for transfers between devices, pointwise_part(): sums = lax.psum((local_up, local_bias, local_down), ('samp', 'vert'))  142 us
    psum x1, blocking collectives, pointwise_part(): sums = lax.psum((local_up, local_bias, local_down), ('samp', 'vert'))  79.6 us
  transfers between devices with their start and end apart: 3, of which 2 were waited for; matrix products, arithmetic and copies ran while one was open for 4% of the time, Pallas kernels for 0%

commit v1 on v0

v1 whole, which is shorter than its diff:
```python
import functools

import jax
import jax.numpy as jnp
from jax import lax
from jax.experimental import pallas as pl
from jax.experimental.pallas import tpu as pltpu
from jax.sharding import Mesh
from jax.sharding import PartitionSpec as P

F32 = jnp.float32
BF16 = jnp.bfloat16
ROOT = 0.7978845608
CUBE = 0.044715
RING = 4
OWNED = 16
SAMP = ("zhi", "core")
VERT = ("x", "zlo", "y")
MIB = 1 << 20


def product(a, b, a_dim, b_dim):
    return lax.dot_general(a, b, (((a_dim,), (b_dim,)), ((), ())), preferred_element_type=F32)


def whole(shape):
    return pl.BlockSpec(shape, lambda *_: (0,) * len(shape))


def project_body(x_at, basis_ref, inputs_ref, cotangent_ref, one, two, three, own, total):
    step = pl.program_id(0)

    @pl.when(step == 0)
    def _():
        total[...] = jnp.zeros_like(total)

    fields = jnp.concatenate(
        [inputs_ref[0], cotangent_ref[0], inputs_ref[1], cotangent_ref[1]], axis=1
    )
    total[...] += product(basis_ref[...], fields, 0, 0)

    @pl.when(step == pl.num_programs(0) - 1)
    def _():
        for shift, out in enumerate((own, one, two, three)):
            first = pl.multiple_of(lax.rem(x_at[0] + shift, RING) * 256, 256)
            out[...] = total[pl.ds(first, 256), :].astype(out.dtype)


def project(x_at, basis, inputs, cotangent, rows=1024):
    field = pl.BlockSpec((2, rows, 128), lambda i, b: (0, i, 0))
    return pl.pallas_call(
        project_body,
        grid_spec=pltpu.PrefetchScalarGridSpec(
            num_scalar_prefetch=1,
            grid=(basis.shape[0] // rows,),
            in_specs=[pl.BlockSpec((rows, 1024), lambda i, b: (i, 0)), field, field],
            out_specs=[whole((256, 512))] * 4,
            scratch_shapes=[pltpu.VMEM((1024, 512), F32)],
        ),
        out_shape=[jax.ShapeDtypeStruct((256, 512), BF16)] * 3
        + [jax.ShapeDtypeStruct((256, 512), F32)],
        compiler_params=pltpu.CompilerParams(vmem_limit_bytes=56 * MIB),
        cost_estimate=pl.CostEstimate(
            flops=2 * 4096 * 1024 * 512, bytes_accessed=13 * MIB, transcendentals=0
        ),
        name="project",
    )(x_at, basis, inputs, cotangent)


def pointwise_body(x_ref, c_ref, up_ref, bias_ref, down_ref, p_ref, gu_ref, gd_ref, gb_ref):
    @pl.when(pl.program_id(0) == 0)
    def _():
        gu_ref[...] = jnp.zeros_like(gu_ref)
        gd_ref[...] = jnp.zeros_like(gd_ref)
        gb_ref[...] = jnp.zeros_like(gb_ref)

    up, down = up_ref[...], down_ref[...]
    x, c = x_ref[...], c_ref[...]
    z = product(x, up, 1, 0) + bias_ref[...]
    square = z * z
    t = jnp.tanh(z * (ROOT + (ROOT * CUBE) * square))
    half = 0.5 * z
    plus = 1.0 + t
    hidden = (half * plus).astype(BF16)
    slope = 0.5 * plus + half * (1.0 - t * t) * (ROOT + (3.0 * CUBE * ROOT) * square)
    grad_pre = (product(c, down, 1, 1) * slope).astype(BF16)
    p_ref[...] = product(grad_pre, up, 1, 1)
    with_ones = jnp.concatenate([x, jnp.ones((x.shape[0], 128), BF16)], axis=1)
    sums = product(with_ones, grad_pre, 0, 0)
    gu_ref[...] += sums[:128]
    gb_ref[...] += sums[128:136]
    gd_ref[...] += product(c, hidden, 0, 0)


def pointwise(x, c, up, bias, down, rows=1024):
    count = x.shape[0] // rows
    moving = pl.BlockSpec((rows, 128), lambda i: (i, 0))
    sums = [(128, 512), (128, 512), (8, 512)]
    return pl.pallas_call(
        pointwise_body,
        grid=(count,),
        in_specs=[moving, moving, whole((128, 512)), whole((1, 512)), whole((512, 128))],
        out_specs=[moving] + [whole(s) for s in sums],
        out_shape=[jax.ShapeDtypeStruct(s, F32) for s in [x.shape] + sums],
        compiler_params=pltpu.CompilerParams(vmem_limit_bytes=52 * MIB),
        cost_estimate=pl.CostEstimate(
            flops=10 * count * rows * 128 * 512,
            bytes_accessed=count * rows * 128 * 8,
            transcendentals=count * rows * 512,
        ),
        name="pointwise",
    )(x, c, up, bias, down)


def pack_body(own, one, two, three, gu, gd, gb, out):
    total = own[...] + one[...].astype(F32) + two[...].astype(F32) + three[...].astype(F32)
    row = lax.broadcasted_iota(jnp.int32, (8, 128), 0)
    bias = jnp.zeros((8, 128), F32)
    for g in range(4):
        bias = jnp.where(row == g, gb[:, g * 128 : (g + 1) * 128], bias)
    bias = jnp.concatenate([bias, jnp.zeros((8, 128), F32)], axis=0).astype(BF16)
    for j in range(16):
        for g in range(4):
            out[j, g * 16 : (g + 1) * 16, :] = total[
                j * 16 : (j + 1) * 16, g * 128 : (g + 1) * 128
            ].astype(BF16)
        for k, ref in enumerate((gu, gd)):
            for q in range(2):
                pair = [
                    ref[j * 8 : (j + 1) * 8, g * 128 : (g + 1) * 128] for g in (2 * q, 2 * q + 1)
                ]
                first = 64 + k * 32 + q * 16
                out[j, first : first + 16, :] = jnp.concatenate(pair, axis=0).astype(BF16)
        out[j, 128:144, :] = bias


def small(body, name, out_shape, *args):
    return pl.pallas_call(
        body,
        out_shape=out_shape,
        compiler_params=pltpu.CompilerParams(vmem_limit_bytes=32 * MIB),
        name=name,
    )(*args)


def own_body(messages, weights, sums_ref, coef_ref):
    sums = messages[0].astype(F32)
    for j in range(1, 16):
        sums = sums + messages[j].astype(F32)
    sums_ref[...] = sums
    parts = []
    for sample in range(2):
        rest = sums[sample * 32 + 16 : sample * 32 + 32]
        for _ in range(3):
            parts.append(rest.astype(BF16))
            rest = rest - parts[-1].astype(F32)
    left = jnp.concatenate(parts, axis=0)
    row = lax.broadcasted_iota(jnp.int32, (16, 128), 0)
    first = jnp.zeros((16, 128), F32)
    second = jnp.zeros((16, 128), F32)
    for k in range(16):
        mixed = product(left, weights[k], 1, 1)
        first = jnp.where(row == k, mixed[0:16] + mixed[16:32] + mixed[32:48], first)
        second = jnp.where(row == k, mixed[48:64] + mixed[64:80] + mixed[80:96], second)
    coef = jnp.concatenate([first, second], axis=1).astype(BF16)
    for v in range(64):
        coef_ref[v] = coef


def finish_body(basis_ref, coef_ref, p_ref, out_ref):
    total = product(basis_ref[...], coef_ref[...], 1, 0)
    out_ref[0] = (total[:, :128] + p_ref[0]).astype(out_ref.dtype)
    out_ref[1] = (total[:, 128:] + p_ref[1]).astype(out_ref.dtype)


def finish(basis, coef, point, rows=1024):
    vertices = basis.shape[0]
    both = pl.BlockSpec((2, rows, 128), lambda i: (0, i, 0))
    return pl.pallas_call(
        finish_body,
        grid=(vertices // rows,),
        in_specs=[pl.BlockSpec((rows, 1024), lambda i: (i, 0)), whole((1024, 256)), both],
        out_specs=both,
        out_shape=jax.ShapeDtypeStruct((2, vertices, 128), BF16),
        compiler_params=pltpu.CompilerParams(vmem_limit_bytes=56 * MIB),
        cost_estimate=pl.CostEstimate(
            flops=2 * vertices * 1024 * 256, bytes_accessed=16 * MIB, transcendentals=0
        ),
        name="finish",
    )(basis, coef, point)


def weights_body(pieces, bias, gu_ref, gd_ref, gb_ref, down):
    for j in range(16):
        for k, ref in enumerate((gu_ref, down)):
            for q in range(2):
                first = k * 32 + q * 16
                pair = pieces[j, first : first + 16, :].astype(F32)
                for h in range(2):
                    g = 2 * q + h
                    ref[j * 8 : (j + 1) * 8, g * 128 : (g + 1) * 128] = pair[h * 8 : (h + 1) * 8]
    gd_ref[...] = down[...].T
    gb_ref[...] = bias[0:4, :]


def flip(value, axis, size, mask):
    return lax.ppermute(value, axis, [(i, i ^ mask) for i in range(size)])


def in_order(axis, mine, theirs):
    low = lax.axis_index(axis) == 0
    return jnp.where(low, mine, theirs), jnp.where(low, theirs, mine)


def per_device(inputs, cotangent, basis, mode_weights, w_up, b_up, w_down):
    x_at = lax.axis_index("x").reshape(1)
    vertices = inputs.shape[1]

    *chunks, own = project(x_at, basis, inputs, cotangent)
    inputs, cotangent, chunks = lax.optimization_barrier((inputs, cotangent, chunks))
    arrived = [
        lax.ppermute(chunks[s - 1], "x", [(i, (i + s) % RING) for i in range(RING)])
        for s in (2, 1, 3)
    ]
    point, gu, gd, gb = pointwise(
        inputs.reshape(-1, 128), cotangent.reshape(-1, 128), w_up, b_up.reshape(1, 512), w_down
    )
    packed = small(
        pack_body, "pack", jax.ShapeDtypeStruct((16, 144, 128), BF16), own, *arrived, gu, gd, gb
    )
    messages = lax.all_to_all(packed, ("zlo", "y"), 0, 0)
    sums, coef = small(
        own_body,
        "own",
        [jax.ShapeDtypeStruct((144, 128), F32), jax.ShapeDtypeStruct((64, OWNED, 256), BF16)],
        messages,
        mode_weights,
    )
    coef = lax.all_to_all(coef, VERT, 0, 0).reshape(1024, 256)
    grad_input = finish(basis, coef, point.reshape(2, vertices, 128))

    other = flip(sums, "core", 2, 1)
    held = jnp.concatenate(in_order("core", sums[:64], other[:64]), axis=0)
    grads = sums[64:] + other[64:]
    other = flip(jnp.concatenate([held, grads], axis=0), "zhi", 2, 1)
    everyone = jnp.concatenate(in_order("zhi", held, other[:128]), axis=0)
    grads = grads + other[128:]
    grads = grads + flip(grads, "x", RING, 1)
    grads = grads + flip(grads, "x", RING, 3)
    pieces = jnp.broadcast_to(grads[:64].astype(BF16)[None], (16, 64, 128))
    pieces = lax.all_to_all(pieces, ("zlo", "y"), 0, 0)
    grad_w_up, grad_w_down, grad_b_up = pl.pallas_call(
        weights_body,
        out_shape=[
            jax.ShapeDtypeStruct((128, 512), F32),
            jax.ShapeDtypeStruct((512, 128), F32),
            jax.ShapeDtypeStruct((4, 128), F32),
        ],
        scratch_shapes=[pltpu.VMEM((128, 512), F32)],
        name="weights",
    )(pieces, grads[64:])

    everyone = everyone.reshape(RING, 2, 2, OWNED, 128)
    grad_modes = jnp.einsum(
        "gskc,gskd->kcd", everyone[:, :, 0], everyone[:, :, 1], precision=lax.Precision.HIGHEST
    )
    return (grad_input, grad_modes, grad_w_up, grad_b_up.reshape(512), grad_w_down)


def solution(mesh):
    fine = Mesh(mesh.devices.reshape(2, 2, RING, RING, RING), SAMP + VERT)
    in_specs = (
        P(SAMP, VERT, None),
        P(SAMP, VERT, None),
        P(VERT, None),
        P(VERT, None, None),
        P(),
        P(),
        P(),
    )
    out_specs = (P(SAMP, VERT, None), P(VERT, None, None), P(), P(), P())
    return jax.shard_map(
        per_device, mesh=fine, in_specs=in_specs, out_specs=out_specs, check_vma=False
    )
```

time: 1230 us -> 123 us (0.10)
  the two profiles are of different devices: /device:TPU:0 before, /device:TPU:8 now
where the time goes in v1:
time: 123 us
  blocking collectives  39.5 us (32%)
  Pallas kernels  38.9 us (32%)
  waiting for transfers between devices  22.9 us (19%)
  starting transfers between devices  16.6 us (13%)
  matrix products  2.81 us (2%)
  local copies, waits for them, and re-layouts  1.47 us (1%)
    all_to_all x1, blocking collectives, per_device(): messages = lax.all_to_all(packed, ('zlo', 'y'), 0, 0)  24.5 us
    pallas_call x1, Pallas kernels, pointwise(): pl.pallas_call(pointwise_body, grid=(count,), in_specs=[moving, moving, w...  19 us
    all_to_all x1, blocking collectives, per_device(): pieces = lax.all_to_all(pieces, ('zlo', 'y'), 0, 0)  14.9 us
    ppermute x4, waiting for transfers between devices, flip(): return lax.ppermute(value, axis, [(i, i ^ mask) for i in range(size)])  14.8 us
    pallas_call x1, Pallas kernels, project(): pl.pallas_call(project_body, grid_spec=pltpu.PrefetchScalarGridSpec(num_s...  9.08 us
    all_to_all x1, waiting for transfers between devices, per_device(): coef = lax.all_to_all(coef, VERT, 0, 0).reshape(1024, 256)  8.18 us
    pallas_call x1, Pallas kernels, finish(): pl.pallas_call(finish_body, grid=(vertices // rows,), in_specs=[pl.BlockS...  7.55 us
    ppermute x3, starting transfers between devices, per_device(): lax.ppermute(chunks[s - 1], 'x', [(i, (i + s) % RING) for i in range(RING)])  6.26 us
  transfers between devices with their start and end apart: 8, of which 5 were waited for; matrix products, arithmetic and copies ran while one was open for 3% of the time, Pallas kernels for 17%

profile of v1, /device:TPU:8, one launch (start us, length us, event | category | flops | bytes accessed | tf_op | source)
XLA Modules:
  0.0 123.0 jit_solution(17987409350799454474)
XLA Ops:
  0.6 0.0 copy-start.2
  0.6 0.0 copy-start.3
  0.7 0.0 copy-start.4
  0.7 9.1 %project.1 = (bf16[256,512]{1,0:T(8,128)(2,1)}, bf16[256,512]{1,0:T(8,128)(2,1)}, bf16[256,512]{1,0:T(8,128)(2,1)}, f32[256,512]{1,0:T(8,128)}) custom-call(s32[1]{0:T(128)} %bitcast.x_at, bf16[4096,1024]{1,0:T(8,128)(2,1)} %basis_ref.3, bf16[2,4096,128]{2,1,0:T(8,128)(2,1)} %inputs_ref.1, bf16[2,4096,128]{2,1,0:T(8,128)(2,1)} %cotangent_ref.1), custom_call_target="tpu_custom_call" | custom-call | flops 4294967296 | bytes 13631488 | tf_op jit(solution)/shard_map/project/pallas_call | solution.py:51
  9.7 3.0 %collective-permute-start = (bf16[256,512]{1,0:T(8,128)(2,1)}, bf16[256,512]{1,0:T(8,128)(2,1)S(1)}, u32[]{:S(2)}, u32[]{:S(2)}) collective-permute-start(bf16[256,512]{1,0:T(8,128)(2,1)} %get-tuple-element.27), channel_id=1, source_target_pairs={{0,32},{16,48},{32,0},{48,16},{1,33},{17,49},{33,1},{49,17},{2,34}... | collective-permute-start | bytes 786440 | tf_op jit(solution)/shard_map/ppermute | solution.py:222
  12.8 0.6 collective-permute-start.1
  13.4 2.6 %collective-permute-start.2 = (bf16[256,512]{1,0:T(8,128)(2,1)}, bf16[256,512]{1,0:T(8,128)(2,1)S(1)}, u32[]{:S(2)}, u32[]{:S(2)}) collective-permute-start(bf16[256,512]{1,0:T(8,128)(2,1)} %get-tuple-element.29), channel_id=1, source_target_pairs={{0,48},{16,0},{32,16},{48,32},{1,49},{17,1},{33,17},{49,33},{2,50}... | collective-permute-start | bytes 786440 | tf_op jit(solution)/shard_map/ppermute | solution.py:222
  16.0 0.0 copy-done.2
  16.0 0.0 copy-done.3
  16.0 0.0 copy-done.4
  16.0 0.0 copy-start
  16.0 19.0 %pointwise.1 = (f32[8192,128]{1,0:T(8,128)}, f32[128,512]{1,0:T(8,128)S(1)}, f32[128,512]{1,0:T(8,128)S(1)}, f32[8,512]{1,0:T(8,128)S(1)}) custom-call(bf16[8192,128]{1,0:T(8,128)(2,1)} %bitcast.21, bf16[8192,128]{1,0:T(8,128)(2,1)} %bitcast.22, bf16[128,512]{1,0:T(8,128)(2,1)S(1)} %copy-done.2, f32[1,512]{1,0:T(1,128)S(1)} %bitcast.17, ...), custom_call_target="tpu_custom_call" | custom-call | flops 5368709120 | bytes 8388608 | tf_op jit(solution)/shard_map/pointwise/pallas_call | solution.py:99
  35.1 0.0 copy-start.1
  35.1 0.0 collective-permute-done.one
  35.1 0.0 collective-permute-done.1.two
  35.1 0.0 collective-permute-done.2.three
  35.1 0.0 copy-done
  35.1 0.1 pack.1
  35.2 24.5 %all_to_all.15.messages = bf16[16,144,128]{2,1,0:T(8,128)(2,1)S(1)} all-to-all(bf16[16,144,128]{2,1,0:T(8,128)(2,1)S(1)} %pack.1), channel_id=1, replica_groups=mesh['zhi'=2,'core'=2,'x'=4,'zlo'=4,'y'=4] {'zlo','y'}, dimensions={0} | all-to-all | bytes 1179648 | tf_op jit(solution)/shard_map/all_to_all | solution.py:231
  59.7 0.0 copy-done.1
  59.7 1.3 %own.1 = (f32[144,128]{1,0:T(8,128)S(1)}, bf16[64,16,256]{2,1,0:T(8,128)(2,1)}) custom-call(bf16[16,144,128]{2,1,0:T(8,128)(2,1)S(1)} %all_to_all.15.messages, bf16[16,128,128]{2,1,0:T(8,128)(2,1)S(1)} %copy-done.1), custom_call_target="tpu_custom_call" | custom-call | tf_op jit(solution)/shard_map/own/pallas_call | solution.py:138
  61.1 0.0 collective-permute-start.3
  61.1 1.3 %collective-permute-done.3 = f32[144,128]{1,0:T(8,128)S(1)} collective-permute-done((f32[144,128]{1,0:T(8,128)S(1)}, f32[144,128]{1,0:T(8,128)S(1)}, u32[]{:S(2)}, u32[]{:S(2)}) %collective-permute-start.3) | collective-permute-done | bytes 73760 | tf_op jit(solution)/shard_map/ppermute | solution.py:207
  62.4 4.6 %collective-permute-start.4 = (f32[208,128]{1,0:T(8,128)S(1)}, f32[208,128]{1,0:T(8,128)S(1)}, u32[]{:S(2)}, u32[]{:S(2)}) collective-permute-start(f32[208,128]{1,0:T(8,128)S(1)} %pad_maximum_fusion.1), channel_id=1, source_target_pairs={{0,128},{128,0},{1,129},{129,1},{2,130},{130,2},{3,131},{131,3},{4... | collective-permute-start | bytes 319496 | tf_op jit(solution)/shard_map/ppermute | solution.py:207
  66.9 4.5 %collective-permute-done.4 = f32[208,128]{1,0:T(8,128)S(1)} collective-permute-done((f32[208,128]{1,0:T(8,128)S(1)}, f32[208,128]{1,0:T(8,128)S(1)}, u32[]{:S(2)}, u32[]{:S(2)}) %collective-permute-start.4) | collective-permute-done | bytes 106528 | tf_op jit(solution)/shard_map/ppermute | solution.py:207
  71.5 0.0 collective-permute-start.5
  71.5 4.0 %collective-permute-done.5 = f32[80,128]{1,0:T(8,128)S(1)} collective-permute-done((f32[80,128]{1,0:T(8,128)S(1)}, f32[80,128]{1,0:T(8,128)S(1)}, u32[]{:S(2)}, u32[]{:S(2)}) %collective-permute-start.5) | collective-permute-done | bytes 40992 | tf_op jit(solution)/shard_map/ppermute | solution.py:207
  75.5 0.3 collective-permute-start.6
  75.8 5.0 %collective-permute-done.6 = f32[80,128]{1,0:T(8,128)S(1)} collective-permute-done((f32[80,128]{1,0:T(8,128)S(1)}, f32[80,128]{1,0:T(8,128)S(1)}, u32[]{:S(2)}, u32[]{:S(2)}) %collective-permute-start.6) | collective-permute-done | bytes 40992 | tf_op jit(solution)/shard_map/ppermute | solution.py:207
  80.8 14.9 %all_to_all.16.pieces = bf16[16,64,128]{2,1,0:T(8,128)(2,1)} all-to-all(bf16[16,64,128]{2,1,0:T(8,128)(2,1)S(1)} %broadcast_in_dim.2), channel_id=1, replica_groups=mesh['zhi'=2,'core'=2,'x'=4,'zlo'=4,'y'=4] {'zlo','y'}, dimensions={0} | all-to-all | bytes 524288 | tf_op jit(solution)/shard_map/all_to_all | solution.py:251
  95.7 5.5 %all-to-all-start.1 = ((bf16[64,16,256]{2,1,0:T(8,128)(2,1)}), bf16[64,16,256]{2,1,0:T(8,128)(2,1)S(1)}, u32[]{:S(2)}, u32[]{:S(2)}) async-start(bf16[64,16,256]{2,1,0:T(8,128)(2,1)} %get-tuple-element.35), calls=%async_computation.1 | async-start | bytes 1048576 | tf_op jit(solution)/shard_map/all_to_all | solution.py:239
  101.3 2.8 %convolution_bitcast_fusion = f32[16,128,128]{2,1,0:T(8,128)} fusion(f32[4,2,1,16,128]{4,3,2,1,0:T(8,128)S(1)} %get-tuple-element.46, f32[4,2,1,16,128]{4,3,2,1,0:T(8,128)S(1)} %get-tuple-element.45), kind=kOutput, calls=%fused_computation | convolution fusion | flops 25165824 | bytes 1179648 | tf_op jit(solution)/shard_map/gskc,gskd->kcd/dot_general | solution.py:264
  104.1 0.6 slice.48.bias
  104.7 1.8 %weights.3 = (f32[128,512]{1,0:T(8,128)}, f32[512,128]{1,0:T(8,128)}, f32[4,128]{1,0:T(4,128)}) custom-call(bf16[16,64,128]{2,1,0:T(8,128)(2,1)} %all_to_all.16.pieces, f32[16,128]{1,0:T(8,128)} %slice.48.bias), custom_call_target="tpu_custom_call" | custom-call | tf_op jit(solution)/shard_map/weights/pallas_call | solution.py:252
  106.5 8.2 %all-to-all-done.1 = bf16[64,16,256]{2,1,0:T(8,128)(2,1)S(1)} async-done(((bf16[64,16,256]{2,1,0:T(8,128)(2,1)}), bf16[64,16,256]{2,1,0:T(8,128)(2,1)S(1)}, u32[]{:S(2)}, u32[]{:S(2)}) %all-to-all-start.1) | async-done | bytes 524320 | tf_op jit(solution)/shard_map/all_to_all | solution.py:239
  114.7 0.0 copy-start.5
  114.7 0.8 copy-done.5
  115.5 7.6 %finish.1 = bf16[2,4096,128]{2,1,0:T(8,128)(2,1)} custom-call(bf16[4096,1024]{1,0:T(8,128)(2,1)} %basis_ref.3, bf16[1024,256]{1,0:T(8,128)(2,1)} %bitcast.19, f32[2,4096,128]{2,1,0:T(8,128)} %bitcast.18), custom_call_target="tpu_custom_call" | custom-call | flops 2147483648 | bytes 16777216 | tf_op jit(solution)/shard_map/finish/pallas_call | solution.py:179
  (11 shorter events, 0.1 us)
Async XLA Ops:
  0.6 15.4 %copy-start.2 = (bf16[128,512]{1,0:T(8,128)(2,1)S(1)}, bf16[128,512]{1,0:T(8,128)(2,1)}, u32[]{:S(2)}) copy-start(bf16[128,512]{1,0:T(8,128)(2,1)} %up_ref.1) | copy-start | bytes 393220
  0.6 15.4 %copy-start.3 = (bf16[512,128]{1,0:T(8,128)(2,1)S(1)}, bf16[512,128]{1,0:T(8,128)(2,1)}, u32[]{:S(2)}) copy-start(bf16[512,128]{1,0:T(8,128)(2,1)} %down_ref.1) | copy-start | bytes 393220
  0.7 15.4 %copy-start.4 = (f32[512]{0:T(512)S(1)}, f32[512]{0:T(512)}, u32[]{:S(2)}) copy-start(f32[512]{0:T(512)} %param.12) | copy-start | bytes 6148
  9.7 25.3 %collective-permute-start = (bf16[256,512]{1,0:T(8,128)(2,1)}, bf16[256,512]{1,0:T(8,128)(2,1)S(1)}, u32[]{:S(2)}, u32[]{:S(2)}) collective-permute-start(bf16[256,512]{1,0:T(8,128)(2,1)} %get-tuple-element.27), channel_id=1, source_target_pairs={{0,32},{16,48},{32,0},{48,16},{1,33},{17,49},{33,1},{49,17},{2,34}... | collective-permute-start | bytes 786440 | tf_op jit(solution)/shard_map/ppermute | solution.py:222
  12.8 22.3 %collective-permute-start.1 = (bf16[256,512]{1,0:T(8,128)(2,1)}, bf16[256,512]{1,0:T(8,128)(2,1)S(1)}, u32[]{:S(2)}, u32[]{:S(2)}) collective-permute-start(bf16[256,512]{1,0:T(8,128)(2,1)} %get-tuple-element.28), channel_id=1, source_target_pairs={{0,16},{16,32},{32,48},{48,0},{1,17},{17,33},{33,49},{49,1},{2,18}... | collective-permute-start | bytes 786440 | tf_op jit(solution)/shard_map/ppermute | solution.py:222
  13.4 21.7 %collective-permute-start.2 = (bf16[256,512]{1,0:T(8,128)(2,1)}, bf16[256,512]{1,0:T(8,128)(2,1)S(1)}, u32[]{:S(2)}, u32[]{:S(2)}) collective-permute-start(bf16[256,512]{1,0:T(8,128)(2,1)} %get-tuple-element.29), channel_id=1, source_target_pairs={{0,48},{16,0},{32,16},{48,32},{1,49},{17,1},{33,17},{49,33},{2,50}... | collective-permute-start | bytes 786440 | tf_op jit(solution)/shard_map/ppermute | solution.py:222
  16.0 19.1 %copy-start = (f32[256,512]{1,0:T(8,128)S(1)}, f32[256,512]{1,0:T(8,128)}, u32[]{:S(2)}) copy-start(f32[256,512]{1,0:T(8,128)} %get-tuple-element.23.own) | copy-start | bytes 1572868
  35.1 24.7 %copy-start.1 = (bf16[16,128,128]{2,1,0:T(8,128)(2,1)S(1)}, bf16[16,128,128]{2,1,0:T(8,128)(2,1)}, u32[]{:S(2)}) copy-start(bf16[16,128,128]{2,1,0:T(8,128)(2,1)} %weights.2) | copy-start | bytes 1572868
  61.1 1.3 %collective-permute-start.3 = (f32[144,128]{1,0:T(8,128)S(1)}, f32[144,128]{1,0:T(8,128)S(1)}, u32[]{:S(2)}, u32[]{:S(2)}) collective-permute-start(f32[144,128]{1,0:T(8,128)S(1)} %get-tuple-element.37), channel_id=1, source_target_pairs={{0,64},{64,0},{1,65},{65,1},{2,66},{66,2},{3,67},{67,3},{4,68},{68... | collective-permute-start | bytes 221192 | tf_op jit(solution)/shard_map/ppermute | solution.py:207
  62.4 9.1 %collective-permute-start.4 = (f32[208,128]{1,0:T(8,128)S(1)}, f32[208,128]{1,0:T(8,128)S(1)}, u32[]{:S(2)}, u32[]{:S(2)}) collective-permute-start(f32[208,128]{1,0:T(8,128)S(1)} %pad_maximum_fusion.1), channel_id=1, source_target_pairs={{0,128},{128,0},{1,129},{129,1},{2,130},{130,2},{3,131},{131,3},{4... | collective-permute-start | bytes 319496 | tf_op jit(solution)/shard_map/ppermute | solution.py:207
  71.5 4.0 %collective-permute-start.5 = (f32[80,128]{1,0:T(8,128)S(1)}, f32[80,128]{1,0:T(8,128)S(1)}, u32[]{:S(2)}, u32[]{:S(2)}) collective-permute-start(f32[80,128]{1,0:T(8,128)S(1)} %slice_add_fusion), channel_id=1, source_target_pairs={{0,16},{16,0},{32,48},{48,32},{1,17},{17,1},{33,49},{49,33},{2,18}... | collective-permute-start | bytes 122888 | tf_op jit(solution)/shard_map/ppermute | solution.py:207
  75.5 5.2 %collective-permute-start.6 = (f32[80,128]{1,0:T(8,128)S(1)}, f32[80,128]{1,0:T(8,128)S(1)}, u32[]{:S(2)}, u32[]{:S(2)}) collective-permute-start(f32[80,128]{1,0:T(8,128)S(1)} %add.14), channel_id=1, source_target_pairs={{0,48},{16,32},{32,16},{48,0},{1,49},{17,33},{33,17},{49,1},{2,50}... | collective-permute-start | bytes 122888 | tf_op jit(solution)/shard_map/ppermute | solution.py:207
  95.7 19.0 %all-to-all-start.1 = ((bf16[64,16,256]{2,1,0:T(8,128)(2,1)}), bf16[64,16,256]{2,1,0:T(8,128)(2,1)S(1)}, u32[]{:S(2)}, u32[]{:S(2)}) async-start(bf16[64,16,256]{2,1,0:T(8,128)(2,1)} %get-tuple-element.35), calls=%async_computation.1 | async-start | bytes 1048576 | tf_op jit(solution)/shard_map/all_to_all | solution.py:239
  114.7 0.8 copy-start.5

commit v2 on v1

v2 whole, which is shorter than its diff:
```python
import functools

import jax
import jax.numpy as jnp
from jax import lax
from jax.experimental import pallas as pl
from jax.experimental.pallas import tpu as pltpu
from jax.sharding import Mesh
from jax.sharding import PartitionSpec as P

F32 = jnp.float32
BF16 = jnp.bfloat16
ROOT = 0.7978845608
CUBE = 0.044715
RING = 4
OWNED = 16
SAMP = ("zhi", "core")
VERT = ("x", "zlo", "y")
MIB = 1 << 20


def product(a, b, a_dim, b_dim):
    return lax.dot_general(a, b, (((a_dim,), (b_dim,)), ((), ())), preferred_element_type=F32)


def whole(shape):
    return pl.BlockSpec(shape, lambda *_: (0,) * len(shape))


def project_body(basis_ref, inputs_ref, cotangent_ref, out, total):
    step = pl.program_id(0)

    @pl.when(step == 0)
    def _():
        total[...] = jnp.zeros_like(total)

    fields = jnp.concatenate(
        [inputs_ref[0], cotangent_ref[0], inputs_ref[1], cotangent_ref[1]], axis=1
    )
    total[...] += product(basis_ref[...], fields, 0, 0)

    @pl.when(step == pl.num_programs(0) - 1)
    def _():
        for x in range(RING):
            for y in range(RING):
                for z in range(RING):
                    first = x * 256 + z * 64 + y * 16
                    out[x * RING + y, z * 16 : (z + 1) * 16, :] = total[
                        first : first + 16, :
                    ].astype(BF16)


def project(basis, inputs, cotangent, rows=1024):
    field = pl.BlockSpec((2, rows, 128), lambda i: (0, i, 0))
    return pl.pallas_call(
        project_body,
        grid=(basis.shape[0] // rows,),
        in_specs=[pl.BlockSpec((rows, 1024), lambda i: (i, 0)), field, field],
        out_specs=whole((16, 64, 512)),
        scratch_shapes=[pltpu.VMEM((1024, 512), F32)],
        out_shape=jax.ShapeDtypeStruct((16, 64, 512), BF16),
        compiler_params=pltpu.CompilerParams(vmem_limit_bytes=56 * MIB),
        cost_estimate=pl.CostEstimate(
            flops=2 * 4096 * 1024 * 512, bytes_accessed=13 * MIB, transcendentals=0
        ),
        name="project",
    )(basis, inputs, cotangent)


def pointwise_body(x_ref, c_ref, up_ref, bias_ref, down_ref, p_ref, gu_ref, gd_ref, gb_ref):
    @pl.when(pl.program_id(0) == 0)
    def _():
        gu_ref[...] = jnp.zeros_like(gu_ref)
        gd_ref[...] = jnp.zeros_like(gd_ref)
        gb_ref[...] = jnp.zeros_like(gb_ref)

    up, down = up_ref[...], down_ref[...]
    x, c = x_ref[...], c_ref[...]
    z = product(x, up, 1, 0) + bias_ref[...]
    square = z * z
    t = jnp.tanh(z * (ROOT + (ROOT * CUBE) * square))
    half = 0.5 * z
    plus = 1.0 + t
    hidden = (half * plus).astype(BF16)
    slope = 0.5 * plus + half * (1.0 - t * t) * (ROOT + (3.0 * CUBE * ROOT) * square)
    grad_pre = (product(c, down, 1, 1) * slope).astype(BF16)
    p_ref[...] = product(grad_pre, up, 1, 1)
    with_ones = jnp.concatenate([x, jnp.ones((x.shape[0], 128), BF16)], axis=1)
    sums = product(with_ones, grad_pre, 0, 0)
    gu_ref[...] += sums[:128]
    gb_ref[...] += sums[128:136]
    gd_ref[...] += product(c, hidden, 0, 0)


def pointwise(x, c, up, bias, down, rows=1024):
    count = x.shape[0] // rows
    moving = pl.BlockSpec((rows, 128), lambda i: (i, 0))
    sums = [(128, 512), (128, 512), (8, 512)]
    return pl.pallas_call(
        pointwise_body,
        grid=(count,),
        in_specs=[moving, moving, whole((128, 512)), whole((1, 512)), whole((512, 128))],
        out_specs=[moving] + [whole(s) for s in sums],
        out_shape=[jax.ShapeDtypeStruct(s, F32) for s in [x.shape] + sums],
        compiler_params=pltpu.CompilerParams(vmem_limit_bytes=52 * MIB),
        cost_estimate=pl.CostEstimate(
            flops=10 * count * rows * 128 * 512,
            bytes_accessed=count * rows * 128 * 8,
            transcendentals=count * rows * 512,
        ),
        name="pointwise",
    )(x, c, up, bias, down)


def pack_body(gu, gd, gb, out):
    row = lax.broadcasted_iota(jnp.int32, (8, 128), 0)
    bias = jnp.zeros((8, 128), F32)
    for g in range(4):
        bias = jnp.where(row == g, gb[:, g * 128 : (g + 1) * 128], bias)
    for j in range(16):
        tiles = [
            ref[j * 8 : (j + 1) * 8, g * 128 : (g + 1) * 128] for ref in (gu, gd) for g in range(4)
        ]
        out[j] = jnp.concatenate(tiles + [bias], axis=0).astype(BF16)


def small(body, name, out_shape, *args, scratch=()):
    return pl.pallas_call(
        body,
        out_shape=out_shape,
        in_specs=[
            pl.BlockSpec(memory_space=pltpu.SMEM if v.dtype == jnp.int32 else pltpu.VMEM)
            for v in args
        ],
        scratch_shapes=list(scratch),
        compiler_params=pltpu.CompilerParams(vmem_limit_bytes=32 * MIB),
        name=name,
    )(*args)


def line_body(z_at, messages, own, one, two, three, total):
    sums = messages[0].astype(F32)
    for j in range(1, 16):
        sums = sums + messages[j].astype(F32)
    total[...] = sums
    for shift, out in enumerate((own, one, two, three)):
        first = pl.multiple_of(lax.rem(z_at[0] + shift, RING) * 16, 16)
        out[...] = total[pl.ds(first, 16), :]


def own_body(own, one, two, three, weights, pieces, modes_ref, line_ref):
    total = (own[...] + two[...]) + (one[...] + three[...])
    for g in range(4):
        modes_ref[g * 16 : (g + 1) * 16, :] = total[:, g * 128 : (g + 1) * 128].astype(BF16)
    grads = pieces[0].astype(F32)
    for j in range(1, 16):
        grads = grads + pieces[j].astype(F32)
    parts = []
    for sample in range(2):
        rest = total[:, sample * 256 + 128 : sample * 256 + 256]
        for _ in range(3):
            parts.append(rest.astype(BF16))
            rest = rest - parts[-1].astype(F32)
    left = jnp.concatenate(parts, axis=0)
    row = lax.broadcasted_iota(jnp.int32, (16, 128), 0)
    first = jnp.zeros((16, 128), F32)
    second = jnp.zeros((16, 128), F32)
    for k in range(16):
        mixed = product(left, weights[k], 1, 1)
        first = jnp.where(row == k, mixed[0:16] + mixed[16:32] + mixed[32:48], first)
        second = jnp.where(row == k, mixed[48:64] + mixed[64:80] + mixed[80:96], second)
    line_ref[...] = jnp.concatenate([first, second, grads], axis=0).astype(BF16)


def gather_body(z_at, own, one, two, three, modes, coef_ref, samp_ref, held):
    for shift, ref in enumerate((own, one, two, three)):
        held[lax.rem(z_at[0] + RING - shift, RING)] = ref[0:32, :]
    coef = held[...].reshape(128, 128)
    for v in range(16):
        coef_ref[v] = coef
    parts = [ref[32:104, :].astype(F32) for ref in (own, one, two, three)]
    grads = (parts[0] + parts[2]) + (parts[1] + parts[3])
    samp_ref[0:64, :] = modes[...]
    samp_ref[64:136, :] = grads.astype(BF16)


def join_body(at, own, core, zhi, both, everyone, bias, message):
    for mask, ref in enumerate((own, core, zhi, both)):
        everyone[jnp.bitwise_xor(at[0], mask)] = ref[0:64, :]
    parts = [ref[64:136, :].astype(F32) for ref in (own, core, zhi, both)]
    grads = (parts[0] + parts[1]) + (parts[2] + parts[3])
    bias[...] = grads[64:72]
    body = grads[0:64].astype(BF16)
    for v in range(16):
        message[v] = body


def finish_body(basis_ref, message_ref, p_ref, out_ref, coef):
    @pl.when(pl.program_id(0) == 0)
    def _():
        for x in range(RING):
            for y in range(RING):
                for z in range(RING):
                    first = x * 256 + z * 64 + y * 16
                    for half in range(2):
                        coef[first : first + 16, half * 128 : (half + 1) * 128] = message_ref[
                            x * RING + y, z * 32 + half * 16 : z * 32 + half * 16 + 16, :
                        ]

    total = product(basis_ref[...], coef[...], 1, 0)
    out_ref[0] = (total[:, :128] + p_ref[0]).astype(out_ref.dtype)
    out_ref[1] = (total[:, 128:] + p_ref[1]).astype(out_ref.dtype)


def finish(basis, message, point, rows=1024):
    vertices = basis.shape[0]
    both = pl.BlockSpec((2, rows, 128), lambda i: (0, i, 0))
    return pl.pallas_call(
        finish_body,
        grid=(vertices // rows,),
        in_specs=[pl.BlockSpec((rows, 1024), lambda i: (i, 0)), whole(message.shape), both],
        out_specs=both,
        out_shape=jax.ShapeDtypeStruct((2, vertices, 128), BF16),
        scratch_shapes=[pltpu.VMEM((1024, 256), BF16)],
        compiler_params=pltpu.CompilerParams(vmem_limit_bytes=56 * MIB),
        cost_estimate=pl.CostEstimate(
            flops=2 * vertices * 1024 * 256, bytes_accessed=16 * MIB, transcendentals=0
        ),
        name="finish",
    )(basis, message, point)


def weights_body(message, gu_ref, gd_ref, down):
    for j in range(16):
        tiles = message[j].astype(F32)
        for k, ref in enumerate((gu_ref, down)):
            for g in range(4):
                first = k * 32 + g * 8
                ref[j * 8 : (j + 1) * 8, g * 128 : (g + 1) * 128] = tiles[first : first + 8]
    gd_ref[...] = down[...].T


def shift(value, axis, by):
    return lax.ppermute(value, axis, [(i, (i + by) % RING) for i in range(RING)])


def per_device(inputs, cotangent, basis, mode_weights, w_up, b_up, w_down):
    z_at = lax.axis_index("zlo").reshape(1)
    samp_at = (lax.axis_index("zhi") * 2 + lax.axis_index("core")).reshape(1)
    vertices = inputs.shape[1]
    struct = jax.ShapeDtypeStruct

    packed = project(basis, inputs, cotangent)
    inputs, cotangent, packed = lax.optimization_barrier((inputs, cotangent, packed))
    messages = lax.all_to_all(packed, ("x", "y"), 0, 0)
    point, gu, gd, gb = pointwise(
        inputs.reshape(-1, 128), cotangent.reshape(-1, 128), w_up, b_up.reshape(1, 512), w_down
    )
    torus = ("x", "y")
    pieces = lax.all_to_all(
        small(pack_body, "pack", struct((16, 72, 128), BF16), gu, gd, gb), torus, 0, 0
    )
    own, *chunks = small(
        line_body, "line", [struct((16, 512), F32)] * 4,
        z_at, messages, scratch=[pltpu.VMEM((64, 512), F32)],
    )
    arrived = [shift(chunks[s - 1], "zlo", s) for s in (1, 2, 3)]
    modes, line = small(
        own_body, "own", [struct((64, 128), BF16), struct((104, 128), BF16)],
        own, *arrived, mode_weights, pieces,
    )
    coef, samp = small(
        gather_body, "gather", [struct((16, 128, 128), BF16), struct((136, 128), BF16)],
        z_at, line, *[shift(line, "zlo", s) for s in (1, 2, 3)], modes,
        scratch=[pltpu.VMEM((RING, 32, 128), BF16)],
    )
    coef = lax.all_to_all(coef, torus, 0, 0)
    core = lax.ppermute(samp, "core", [(0, 1), (1, 0)])
    zhi = lax.ppermute(samp, "zhi", [(0, 1), (1, 0)])
    both = lax.ppermute(samp, SAMP, [(i, 3 - i) for i in range(RING)])
    everyone, bias, message = small(
        join_body, "join",
        [struct((RING, 64, 128), BF16), struct((8, 128), F32), struct((16, 64, 128), BF16)],
        samp_at, samp, core, zhi, both,
    )
    coef, message = lax.optimization_barrier((coef, message))
    message = lax.all_to_all(message, torus, 0, 0)
    grad_input = finish(basis, coef, point.reshape(2, vertices, 128))
    grad_w_up, grad_w_down = small(
        weights_body, "weights", [struct((128, 512), F32), struct((512, 128), F32)],
        message, scratch=[pltpu.VMEM((128, 512), F32)],
    )
    everyone = everyone.reshape(RING, 2, 2, OWNED, 128)
    grad_modes = jnp.einsum(
        "gskc,gskd->kcd", everyone[:, :, 0], everyone[:, :, 1], preferred_element_type=F32
    )
    return (grad_input, grad_modes, grad_w_up, bias[:4].reshape(512), grad_w_down)


def solution(mesh):
    fine = Mesh(mesh.devices.reshape(2, 2, RING, RING, RING), SAMP + VERT)
    in_specs = (
        P(SAMP, VERT, None),
        P(SAMP, VERT, None),
        P(VERT, None),
        P(VERT, None, None),
        P(),
        P(),
        P(),
    )
    out_specs = (P(SAMP, VERT, None), P(VERT, None, None), P(), P(), P())
    return jax.shard_map(
        per_device, mesh=fine, in_specs=in_specs, out_specs=out_specs, check_vma=False
    )
```

time: 123 us -> 102 us (0.83)
  the two profiles are of different devices: /device:TPU:8 before, /device:TPU:1 now
where the time goes in v2:
time: 102 us; the launch traced here: 101 us
  starting transfers between devices  45.9 us (45%)
  Pallas kernels  39.3 us (39%)
  waiting for transfers between devices  13.6 us (13%)
  matrix products  1.35 us (1%)
    pallas_call x1, Pallas kernels, pointwise(): pl.pallas_call(pointwise_body, grid=(count,), in_specs=[moving, moving, w...  18.8 us
    ppermute x1, starting transfers between devices, per_device(): both = lax.ppermute(samp, SAMP, [(i, 3 - i) for i in range(RING)])  10.2 us
    ppermute x6, starting transfers between devices, shift(): lax.ppermute(value, axis, [(i, (i + by) % RING) for i in range(RING)])  9.16 us
    pallas_call x1, Pallas kernels, project(): pl.pallas_call(project_body, grid=(basis.shape[0] // rows,), in_specs=[pl...  8.91 us
    all_to_all x1, starting transfers between devices, per_device(): messages = lax.all_to_all(packed, ('x', 'y'), 0, 0)  7.73 us
    pallas_call x1, Pallas kernels, finish(): pl.pallas_call(finish_body, grid=(vertices // rows,), in_specs=[pl.BlockS...  7.66 us
    all_to_all x1, starting transfers between devices, per_device(): message = lax.all_to_all(message, torus, 0, 0)  6.86 us
    all_to_all x1, starting transfers between devices, per_device(): lax.all_to_all(small(pack_body, 'pack', struct((16, 72, 128), BF16), gu,...  6.64 us
  transfers between devices with their start and end apart: 13, of which 7 were waited for; matrix products, arithmetic and copies ran while one was open for 2% of the time, Pallas kernels for 28%

profile of v2, /device:TPU:1, one launch (start us, length us, event | category | flops | bytes accessed | tf_op | source)
XLA Modules:
  0.0 101.4 jit_solution(14324220128489399295)
XLA Ops:
  0.6 8.9 %project.1 = bf16[16,64,512]{2,1,0:T(8,128)(2,1)} custom-call(bf16[4096,1024]{1,0:T(8,128)(2,1)} %basis_ref.3, bf16[2,4096,128]{2,1,0:T(8,128)(2,1)} %inputs_ref.1, bf16[2,4096,128]{2,1,0:T(8,128)(2,1)} %cotangent_ref.1), custom_call_target="tpu_custom_call" | custom-call | flops 4294967296 | bytes 13631488 | tf_op jit(solution)/shard_map/project/pallas_call | solution.py:55
  9.5 0.0 copy-start.1
  9.5 0.0 copy-start.2
  9.5 0.0 copy-start.3
  9.5 7.7 %all-to-all-start = ((bf16[16,64,512]{2,1,0:T(8,128)(2,1)}), bf16[16,64,512]{2,1,0:T(8,128)(2,1)S(1)}, u32[]{:S(2)}, u32[]{:S(2)}) async-start(bf16[16,64,512]{2,1,0:T(8,128)(2,1)} %project.1), calls=%async_computation | async-start | bytes 2097152 | tf_op jit(solution)/shard_map/all_to_all | solution.py:255
  17.3 0.0 copy-done.1
  17.3 0.0 copy-done.2
  17.3 0.0 copy-done.3
  17.3 18.8 %pointwise.1 = (f32[8192,128]{1,0:T(8,128)}, f32[128,512]{1,0:T(8,128)S(1)}, f32[128,512]{1,0:T(8,128)S(1)}, f32[8,512]{1,0:T(8,128)S(1)}) custom-call(bf16[8192,128]{1,0:T(8,128)(2,1)} %bitcast.21, bf16[8192,128]{1,0:T(8,128)(2,1)} %bitcast.22, bf16[128,512]{1,0:T(8,128)(2,1)S(1)} %copy-done.1, f32[1,512]{1,0:T(1,128)S(1)} %bitcast.19, ...), custom_call_target="tpu_custom_call" | custom-call | flops 5368709120 | bytes 8388608 | tf_op jit(solution)/shard_map/pointwise/pallas_call | solution.py:99
  36.2 0.0 copy-start
  36.2 0.7 pack.1
  36.9 0.0 all-to-all-done.messages
  36.9 6.6 %all-to-all-start.1 = ((bf16[16,72,128]{2,1,0:T(8,128)(2,1)}), bf16[16,72,128]{2,1,0:T(8,128)(2,1)S(1)}, u32[]{:S(2)}, u32[]{:S(2)}) async-start(bf16[16,72,128]{2,1,0:T(8,128)(2,1)} %pack.1), calls=%async_computation.1 | async-start | bytes 589824 | tf_op jit(solution)/shard_map/all_to_all | solution.py:260
  43.6 0.2 line.1
  43.7 1.7 %collective-permute-start = (f32[16,512]{1,0:T(8,128)S(1)}, f32[16,512]{1,0:T(8,128)S(1)}, u32[]{:S(2)}, u32[]{:S(2)}) collective-permute-start(f32[16,512]{1,0:T(8,128)S(1)} %get-tuple-element.29), channel_id=1, source_target_pairs={{0,4},{4,8},{8,12},{12,0},{1,5},{5,9},{9,13},{13,1},{2,6},{6,10},{... | collective-permute-start | bytes 98312 | tf_op jit(solution)/shard_map/ppermute | solution.py:244
  45.4 3.0 %collective-permute-start.1 = (f32[16,512]{1,0:T(8,128)S(1)}, f32[16,512]{1,0:T(8,128)S(1)}, u32[]{:S(2)}, u32[]{:S(2)}) collective-permute-start(f32[16,512]{1,0:T(8,128)S(1)} %get-tuple-element.30), channel_id=1, source_target_pairs={{0,8},{4,12},{8,0},{12,4},{1,9},{5,13},{9,1},{13,5},{2,10},{6,14},... | collective-permute-start | bytes 98312 | tf_op jit(solution)/shard_map/ppermute | solution.py:244
  48.4 0.7 collective-permute-start.2
  49.2 1.9 %all-to-all-done.1.pieces = bf16[16,72,128]{2,1,0:T(8,128)(2,1)S(1)} async-done(((bf16[16,72,128]{2,1,0:T(8,128)(2,1)}), bf16[16,72,128]{2,1,0:T(8,128)(2,1)S(1)}, u32[]{:S(2)}, u32[]{:S(2)}) %all-to-all-start.1) | async-done | bytes 294944 | tf_op jit(solution)/shard_map/all_to_all | solution.py:260
  51.1 0.0 collective-permute-done.one
  51.1 0.0 collective-permute-done.1.two
  51.1 1.1 %collective-permute-done.2.three = f32[16,512]{1,0:T(8,128)S(1)} collective-permute-done((f32[16,512]{1,0:T(8,128)S(1)}, f32[16,512]{1,0:T(8,128)S(1)}, u32[]{:S(2)}, u32[]{:S(2)}) %collective-permute-start.2) | collective-permute-done | bytes 32800 | tf_op jit(solution)/shard_map/ppermute | solution.py:244
  52.2 0.0 copy-done
  52.2 0.5 own.1
  52.7 3.4 %collective-permute-start.5 = (bf16[104,128]{1,0:T(8,128)(2,1)S(1)}, bf16[104,128]{1,0:T(8,128)(2,1)S(1)}, u32[]{:S(2)}, u32[]{:S(2)}) collective-permute-start(bf16[104,128]{1,0:T(8,128)(2,1)S(1)} %get-tuple-element.37.own), channel_id=1, source_target_pairs={{0,12},{4,0},{8,4},{12,8},{1,13},{5,1},{9,5},{13,9},{2,14},{6,2},{... | collective-permute-start | bytes 79880 | tf_op jit(solution)/shard_map/ppermute | solution.py:244
  56.0 0.0 collective-permute-start.4
  56.0 0.4 collective-permute-start.3
  56.4 0.6 collective-permute-done.5.three
  57.0 2.6 %collective-permute-done.4.two = bf16[104,128]{1,0:T(8,128)(2,1)S(1)} collective-permute-done((bf16[104,128]{1,0:T(8,128)(2,1)S(1)}, bf16[104,128]{1,0:T(8,128)(2,1)S(1)}, u32[]{:S(2)}, u32[]{:S(2)}) %collective-permute-start.4) | collective-permute-done | bytes 26656 | tf_op jit(solution)/shard_map/ppermute | solution.py:244
  59.6 1.2 %collective-permute-done.3.one = bf16[104,128]{1,0:T(8,128)(2,1)S(1)} collective-permute-done((bf16[104,128]{1,0:T(8,128)(2,1)S(1)}, bf16[104,128]{1,0:T(8,128)(2,1)S(1)}, u32[]{:S(2)}, u32[]{:S(2)}) %collective-permute-start.3) | collective-permute-done | bytes 26656 | tf_op jit(solution)/shard_map/ppermute | solution.py:244
  60.8 0.9 gather.1
  61.7 4.8 %all-to-all-start.2 = ((bf16[16,128,128]{2,1,0:T(8,128)(2,1)}), bf16[16,128,128]{2,1,0:T(8,128)(2,1)S(1)}, u32[]{:S(2)}, u32[]{:S(2)}) async-start(bf16[16,128,128]{2,1,0:T(8,128)(2,1)} %get-tuple-element.39), calls=%async_computation.2 | async-start | bytes 1048576 | tf_op jit(solution)/shard_map/all_to_all | solution.py:277
  66.5 10.2 %collective-permute-start.8 = (bf16[136,128]{1,0:T(8,128)(2,1)S(1)}, bf16[136,128]{1,0:T(8,128)(2,1)S(1)}, u32[]{:S(2)}, u32[]{:S(2)}) collective-permute-start(bf16[136,128]{1,0:T(8,128)(2,1)S(1)} %get-tuple-element.40.own), channel_id=1, source_target_pairs={{0,192},{64,128},{128,64},{192,0},{1,193},{65,129},{129,65},{193,1... | collective-permute-start | bytes 104456 | tf_op jit(solution)/shard_map/ppermute | solution.py:280
  76.6 0.2 collective-permute-start.7
  76.9 0.2 collective-permute-start.6
  77.1 1.7 %collective-permute-done.8.both = bf16[136,128]{1,0:T(8,128)(2,1)S(1)} collective-permute-done((bf16[136,128]{1,0:T(8,128)(2,1)S(1)}, bf16[136,128]{1,0:T(8,128)(2,1)S(1)}, u32[]{:S(2)}, u32[]{:S(2)}) %collective-permute-start.8) | collective-permute-done | bytes 34848 | tf_op jit(solution)/shard_map/ppermute | solution.py:280
  78.9 4.5 %collective-permute-done.7.zhi = bf16[136,128]{1,0:T(8,128)(2,1)S(1)} collective-permute-done((bf16[136,128]{1,0:T(8,128)(2,1)S(1)}, bf16[136,128]{1,0:T(8,128)(2,1)S(1)}, u32[]{:S(2)}, u32[]{:S(2)}) %collective-permute-start.7) | collective-permute-done | bytes 34848 | tf_op jit(solution)/shard_map/ppermute | solution.py:279
  83.3 0.0 collective-permute-done.6.core
  83.3 0.7 join.1
  84.1 0.6 slice_bitcast_fusion
  84.7 0.0 all-to-all-done.2.message_ref
  84.7 0.0 copy-start.4
  84.7 6.9 %all-to-all-start.3 = ((bf16[16,64,128]{2,1,0:T(8,128)(2,1)}), bf16[16,64,128]{2,1,0:T(8,128)(2,1)S(1)}, u32[]{:S(2)}, u32[]{:S(2)}) async-start(bf16[16,64,128]{2,1,0:T(8,128)(2,1)} %get-tuple-element.45), calls=%async_computation.3 | async-start | bytes 524288 | tf_op jit(solution)/shard_map/all_to_all | solution.py:287
  91.6 1.3 %convolution_bitcast_fusion = f32[16,128,128]{2,1,0:T(8,128)} fusion(bf16[4,2,1,16,128]{4,3,2,1,0:T(8,128)(2,1)S(1)} %get-tuple-element.50, bf16[4,2,1,16,128]{4,3,2,1,0:T(8,128)(2,1)S(1)} %get-tuple-element.49), kind=kOutput, calls=%fused_computation | convolution fusion | flops 4194304 | bytes 1114112 | tf_op jit(solution)/shard_map/gskc,gskd->kcd/dot_general | solution.py:294
  92.9 0.0 copy-done.4
  92.9 7.7 %finish.1 = bf16[2,4096,128]{2,1,0:T(8,128)(2,1)} custom-call(bf16[4096,1024]{1,0:T(8,128)(2,1)} %basis_ref.3, bf16[16,128,128]{2,1,0:T(8,128)(2,1)} %copy-done.4, f32[2,4096,128]{2,1,0:T(8,128)} %bitcast.20), custom_call_target="tpu_custom_call" | custom-call | flops 2147483648 | bytes 16777216 | tf_op jit(solution)/shard_map/finish/pallas_call | solution.py:218
  100.6 0.0 all-to-all-done.3.message
  100.6 0.8 weights.3
  (1 shorter events, 0.0 us)
Async XLA Ops:
  9.5 7.7 %copy-start.1 = (bf16[128,512]{1,0:T(8,128)(2,1)S(1)}, bf16[128,512]{1,0:T(8,128)(2,1)}, u32[]{:S(2)}) copy-start(bf16[128,512]{1,0:T(8,128)(2,1)} %up_ref.1) | copy-start | bytes 393220
  9.5 7.8 %copy-start.2 = (bf16[512,128]{1,0:T(8,128)(2,1)S(1)}, bf16[512,128]{1,0:T(8,128)(2,1)}, u32[]{:S(2)}) copy-start(bf16[512,128]{1,0:T(8,128)(2,1)} %down_ref.1) | copy-start | bytes 393220
  9.5 7.8 %copy-start.3 = (f32[512]{0:T(512)S(1)}, f32[512]{0:T(512)}, u32[]{:S(2)}) copy-start(f32[512]{0:T(512)} %param.12) | copy-start | bytes 6148
  9.5 27.4 %all-to-all-start = ((bf16[16,64,512]{2,1,0:T(8,128)(2,1)}), bf16[16,64,512]{2,1,0:T(8,128)(2,1)S(1)}, u32[]{:S(2)}, u32[]{:S(2)}) async-start(bf16[16,64,512]{2,1,0:T(8,128)(2,1)} %project.1), calls=%async_computation | async-start | bytes 2097152 | tf_op jit(solution)/shard_map/all_to_all | solution.py:255
  36.2 16.0 %copy-start = (bf16[16,128,128]{2,1,0:T(8,128)(2,1)S(1)}, bf16[16,128,128]{2,1,0:T(8,128)(2,1)}, u32[]{:S(2)}) copy-start(bf16[16,128,128]{2,1,0:T(8,128)(2,1)} %weights.2) | copy-start | bytes 1572868
  36.9 14.2 %all-to-all-start.1 = ((bf16[16,72,128]{2,1,0:T(8,128)(2,1)}), bf16[16,72,128]{2,1,0:T(8,128)(2,1)S(1)}, u32[]{:S(2)}, u32[]{:S(2)}) async-start(bf16[16,72,128]{2,1,0:T(8,128)(2,1)} %pack.1), calls=%async_computation.1 | async-start | bytes 589824 | tf_op jit(solution)/shard_map/all_to_all | solution.py:260
  43.7 7.4 %collective-permute-start = (f32[16,512]{1,0:T(8,128)S(1)}, f32[16,512]{1,0:T(8,128)S(1)}, u32[]{:S(2)}, u32[]{:S(2)}) collective-permute-start(f32[16,512]{1,0:T(8,128)S(1)} %get-tuple-element.29), channel_id=1, source_target_pairs={{0,4},{4,8},{8,12},{12,0},{1,5},{5,9},{9,13},{13,1},{2,6},{6,10},{... | collective-permute-start | bytes 98312 | tf_op jit(solution)/shard_map/ppermute | solution.py:244
  45.4 5.7 %collective-permute-start.1 = (f32[16,512]{1,0:T(8,128)S(1)}, f32[16,512]{1,0:T(8,128)S(1)}, u32[]{:S(2)}, u32[]{:S(2)}) collective-permute-start(f32[16,512]{1,0:T(8,128)S(1)} %get-tuple-element.30), channel_id=1, source_target_pairs={{0,8},{4,12},{8,0},{12,4},{1,9},{5,13},{9,1},{13,5},{2,10},{6,14},... | collective-permute-start | bytes 98312 | tf_op jit(solution)/shard_map/ppermute | solution.py:244
  48.4 3.7 %collective-permute-start.2 = (f32[16,512]{1,0:T(8,128)S(1)}, f32[16,512]{1,0:T(8,128)S(1)}, u32[]{:S(2)}, u32[]{:S(2)}) collective-permute-start(f32[16,512]{1,0:T(8,128)S(1)} %get-tuple-element.31), channel_id=1, source_target_pairs={{0,12},{4,0},{8,4},{12,8},{1,13},{5,1},{9,5},{13,9},{2,14},{6,2},{... | collective-permute-start | bytes 98312 | tf_op jit(solution)/shard_map/ppermute | solution.py:244
  52.7 4.3 %collective-permute-start.5 = (bf16[104,128]{1,0:T(8,128)(2,1)S(1)}, bf16[104,128]{1,0:T(8,128)(2,1)S(1)}, u32[]{:S(2)}, u32[]{:S(2)}) collective-permute-start(bf16[104,128]{1,0:T(8,128)(2,1)S(1)} %get-tuple-element.37.own), channel_id=1, source_target_pairs={{0,12},{4,0},{8,4},{12,8},{1,13},{5,1},{9,5},{13,9},{2,14},{6,2},{... | collective-permute-start | bytes 79880 | tf_op jit(solution)/shard_map/ppermute | solution.py:244
  56.0 3.6 %collective-permute-start.4 = (bf16[104,128]{1,0:T(8,128)(2,1)S(1)}, bf16[104,128]{1,0:T(8,128)(2,1)S(1)}, u32[]{:S(2)}, u32[]{:S(2)}) collective-permute-start(bf16[104,128]{1,0:T(8,128)(2,1)S(1)} %get-tuple-element.37.own), channel_id=1, source_target_pairs={{0,8},{4,12},{8,0},{12,4},{1,9},{5,13},{9,1},{13,5},{2,10},{6,14},... | collective-permute-start | bytes 79880 | tf_op jit(solution)/shard_map/ppermute | solution.py:244
  56.0 4.8 %collective-permute-start.3 = (bf16[104,128]{1,0:T(8,128)(2,1)S(1)}, bf16[104,128]{1,0:T(8,128)(2,1)S(1)}, u32[]{:S(2)}, u32[]{:S(2)}) collective-permute-start(bf16[104,128]{1,0:T(8,128)(2,1)S(1)} %get-tuple-element.37.own), channel_id=1, source_target_pairs={{0,4},{4,8},{8,12},{12,0},{1,5},{5,9},{9,13},{13,1},{2,6},{6,10},{... | collective-permute-start | bytes 79880 | tf_op jit(solution)/shard_map/ppermute | solution.py:244
  61.7 23.0 %all-to-all-start.2 = ((bf16[16,128,128]{2,1,0:T(8,128)(2,1)}), bf16[16,128,128]{2,1,0:T(8,128)(2,1)S(1)}, u32[]{:S(2)}, u32[]{:S(2)}) async-start(bf16[16,128,128]{2,1,0:T(8,128)(2,1)} %get-tuple-element.39), calls=%async_computation.2 | async-start | bytes 1048576 | tf_op jit(solution)/shard_map/all_to_all | solution.py:277
  66.5 12.4 %collective-permute-start.8 = (bf16[136,128]{1,0:T(8,128)(2,1)S(1)}, bf16[136,128]{1,0:T(8,128)(2,1)S(1)}, u32[]{:S(2)}, u32[]{:S(2)}) collective-permute-start(bf16[136,128]{1,0:T(8,128)(2,1)S(1)} %get-tuple-element.40.own), channel_id=1, source_target_pairs={{0,192},{64,128},{128,64},{192,0},{1,193},{65,129},{129,65},{193,1... | collective-permute-start | bytes 104456 | tf_op jit(solution)/shard_map/ppermute | solution.py:280
  76.6 6.7 %collective-permute-start.7 = (bf16[136,128]{1,0:T(8,128)(2,1)S(1)}, bf16[136,128]{1,0:T(8,128)(2,1)S(1)}, u32[]{:S(2)}, u32[]{:S(2)}) collective-permute-start(bf16[136,128]{1,0:T(8,128)(2,1)S(1)} %get-tuple-element.40.own), channel_id=1, source_target_pairs={{0,128},{128,0},{1,129},{129,1},{2,130},{130,2},{3,131},{131,3},{4... | collective-permute-start | bytes 104456 | tf_op jit(solution)/shard_map/ppermute | solution.py:279
  76.9 6.5 %collective-permute-start.6 = (bf16[136,128]{1,0:T(8,128)(2,1)S(1)}, bf16[136,128]{1,0:T(8,128)(2,1)S(1)}, u32[]{:S(2)}, u32[]{:S(2)}) collective-permute-start(bf16[136,128]{1,0:T(8,128)(2,1)S(1)} %get-tuple-element.40.own), channel_id=1, source_target_pairs={{0,64},{64,0},{1,65},{65,1},{2,66},{66,2},{3,67},{67,3},{4,68},{68... | collective-permute-start | bytes 104456 | tf_op jit(solution)/shard_map/ppermute | solution.py:278
  84.7 8.2 %copy-start.4 = (bf16[16,128,128]{2,1,0:T(8,128)(2,1)}, bf16[16,128,128]{2,1,0:T(8,128)(2,1)S(1)}, u32[]{:S(2)}) copy-start(bf16[16,128,128]{2,1,0:T(8,128)(2,1)S(1)} %all-to-all-done.2.message_ref) | copy-start | bytes 1572868
  84.7 15.9 %all-to-all-start.3 = ((bf16[16,64,128]{2,1,0:T(8,128)(2,1)}), bf16[16,64,128]{2,1,0:T(8,128)(2,1)S(1)}, u32[]{:S(2)}, u32[]{:S(2)}) async-start(bf16[16,64,128]{2,1,0:T(8,128)(2,1)} %get-tuple-element.45), calls=%async_computation.3 | async-start | bytes 524288 | tf_op jit(solution)/shard_map/all_to_all | solution.py:287

commit v3 on v2

--- a/solution.py
+++ b/solution.py
@@ -23,42 +23,61 @@
     return lax.dot_general(a, b, (((a_dim,), (b_dim,)), ((), ())), preferred_element_type=F32)
 
 
-def whole(shape):
-    return pl.BlockSpec(shape, lambda *_: (0,) * len(shape))
-
-
-def project_body(basis_ref, inputs_ref, cotangent_ref, out, total):
-    step = pl.program_id(0)
-
-    @pl.when(step == 0)
-    def _():
-        total[...] = jnp.zeros_like(total)
-
-    fields = jnp.concatenate(
-        [inputs_ref[0], cotangent_ref[0], inputs_ref[1], cotangent_ref[1]], axis=1
-    )
-    total[...] += product(basis_ref[...], fields, 0, 0)
-
-    @pl.when(step == pl.num_programs(0) - 1)
-    def _():
-        for x in range(RING):
-            for y in range(RING):
-                for z in range(RING):
-                    first = x * 256 + z * 64 + y * 16
-                    out[x * RING + y, z * 16 : (z + 1) * 16, :] = total[
-                        first : first + 16, :
-                    ].astype(BF16)
-
-
-def project(basis, inputs, cotangent, rows=1024):
-    field = pl.BlockSpec((2, rows, 128), lambda i: (0, i, 0))
+PIECES = 8
+AHEAD = 3
+VMEM = pl.BlockSpec(memory_space=pltpu.VMEM)
+HBM = pl.BlockSpec(memory_space=pltpu.HBM)
+
+
+def project_body(basis_hbm, x_hbm, c_hbm, out, basis, x, c, total, sems):
+    rows = basis.shape[0] // PIECES
+
+    def copies(i):
+        at = pl.ds(i * rows, rows)
+        return [
+            pltpu.make_async_copy(basis_hbm.at[at], basis.at[at], sems.at[0, i]),
+            pltpu.make_async_copy(x_hbm.at[:, at], x.at[:, at], sems.at[1, i]),
+            pltpu.make_async_copy(c_hbm.at[:, at], c.at[:, at], sems.at[2, i]),
+        ]
+
+    for i in range(AHEAD):
+        for copy in copies(i):
+            copy.start()
+    for i in range(PIECES):
+        for copy in copies(i):
+            copy.wait()
+        if i + AHEAD < PIECES:
+            for copy in copies(i + AHEAD):
+                copy.start()
+        at = slice(i * rows, (i + 1) * rows)
+        fields = jnp.concatenate([x[0, at], c[0, at], x[1, at], c[1, at]], axis=1)
+        part = product(basis[at], fields, 0, 0)
+        if i == 0:
+            total[...] = part
+        else:
+            total[...] += part
+    for x_at in range(RING):
+        for y in range(RING):
+            for z in range(RING):
+                first = x_at * 256 + z * 64 + y * 16
+                out[x_at * RING + y, z * 16 : (z + 1) * 16, :] = total[
+                    first : first + 16, :
+                ].astype(BF16)
+
+
+def project(basis, inputs, cotangent):
     return pl.pallas_call(
         project_body,
-        grid=(basis.shape[0] // rows,),
-        in_specs=[pl.BlockSpec((rows, 1024), lambda i: (i, 0)), field, field],
-        out_specs=whole((16, 64, 512)),
-        scratch_shapes=[pltpu.VMEM((1024, 512), F32)],
+        in_specs=[HBM] * 3,
+        out_specs=VMEM,
         out_shape=jax.ShapeDtypeStruct((16, 64, 512), BF16),
+        scratch_shapes=[
+            pltpu.VMEM(basis.shape, BF16),
+            pltpu.VMEM(inputs.shape, BF16),
+            pltpu.VMEM(cotangent.shape, BF16),
+            pltpu.VMEM((1024, 512), F32),
+            pltpu.SemaphoreType.DMA((3, PIECES)),
+        ],
         compiler_params=pltpu.CompilerParams(vmem_limit_bytes=56 * MIB),
         cost_estimate=pl.CostEstimate(
             flops=2 * 4096 * 1024 * 512, bytes_accessed=13 * MIB, transcendentals=0
@@ -67,46 +86,76 @@
     )(basis, inputs, cotangent)
 
 
-def pointwise_body(x_ref, c_ref, up_ref, bias_ref, down_ref, p_ref, gu_ref, gd_ref, gb_ref):
-    @pl.when(pl.program_id(0) == 0)
-    def _():
-        gu_ref[...] = jnp.zeros_like(gu_ref)
-        gd_ref[...] = jnp.zeros_like(gd_ref)
-        gb_ref[...] = jnp.zeros_like(gb_ref)
-
-    up, down = up_ref[...], down_ref[...]
-    x, c = x_ref[...], c_ref[...]
-    z = product(x, up, 1, 0) + bias_ref[...]
-    square = z * z
-    t = jnp.tanh(z * (ROOT + (ROOT * CUBE) * square))
-    half = 0.5 * z
-    plus = 1.0 + t
-    hidden = (half * plus).astype(BF16)
-    slope = 0.5 * plus + half * (1.0 - t * t) * (ROOT + (3.0 * CUBE * ROOT) * square)
-    grad_pre = (product(c, down, 1, 1) * slope).astype(BF16)
-    p_ref[...] = product(grad_pre, up, 1, 1)
-    with_ones = jnp.concatenate([x, jnp.ones((x.shape[0], 128), BF16)], axis=1)
-    sums = product(with_ones, grad_pre, 0, 0)
-    gu_ref[...] += sums[:128]
-    gb_ref[...] += sums[128:136]
-    gd_ref[...] += product(c, hidden, 0, 0)
-
-
-def pointwise(x, c, up, bias, down, rows=1024):
-    count = x.shape[0] // rows
-    moving = pl.BlockSpec((rows, 128), lambda i: (i, 0))
-    sums = [(128, 512), (128, 512), (8, 512)]
+def pointwise_body(
+    x_hbm, c_hbm, up_ref, bias_ref, down_ref, p_hbm, gu_ref, gd_ref, gb_ref, x_ref, c_ref, p_ref, sems
+):
+    rows = 2048
+    count = x_ref.shape[0] // rows
+
+    def copy(k, i, at):
+        if k == 2:
+            return pltpu.make_async_copy(p_ref.at[at], p_hbm.at[at], sems.at[2, i])
+        source, held = ((x_hbm, x_ref), (c_hbm, c_ref))[k]
+        return pltpu.make_async_copy(source.at[at], held.at[at], sems.at[k, i])
+
+    def load(i):
+        at = pl.ds(pl.multiple_of(i * rows, rows), rows)
+        copy(0, i, at).start()
+        copy(1, i, at).start()
+
+    load(0)
+    gu_ref[...] = jnp.zeros_like(gu_ref)
+    gd_ref[...] = jnp.zeros_like(gd_ref)
+    gb_ref[...] = jnp.zeros_like(gb_ref)
+
+    @pl.loop(0, count)
+    def _(i):
+        at = pl.ds(pl.multiple_of(i * rows, rows), rows)
+        copy(0, i, at).wait()
+        copy(1, i, at).wait()
+
+        @pl.when(i + 1 < count)
+        def _():
+            load(i + 1)
+
+        up, down = up_ref[...], down_ref[...]
+        x, c = x_ref[at, :], c_ref[at, :]
+        z = product(x, up, 1, 0) + bias_ref[...]
+        square = z * z
+        q = 0.5 + 0.5 * jnp.tanh(z * (ROOT + (ROOT * CUBE) * square))
+        value = z * q
+        hidden = value.astype(BF16)
+        slope = q + (value - value * q) * (2.0 * ROOT + (6.0 * CUBE * ROOT) * square)
+        grad_pre = (product(c, down, 1, 1) * slope).astype(BF16)
+        p_ref[at, :] = product(grad_pre, up, 1, 1).astype(BF16)
+        copy(2, i, at).start()
+        with_ones = jnp.concatenate([x, jnp.ones((rows, 128), BF16)], axis=1)
+        sums = product(with_ones, grad_pre, 0, 0)
+        gu_ref[...] += sums[:128]
+        gb_ref[...] += sums[128:136]
+        gd_ref[...] += product(c, hidden, 0, 0)
+
+    for i in range(count):
+        copy(2, i, pl.ds(i * rows, rows)).wait()
+
+
+def pointwise(x, c, up, bias, down):
+    rows = x.shape[0]
     return pl.pallas_call(
         pointwise_body,
-        grid=(count,),
-        in_specs=[moving, moving, whole((128, 512)), whole((1, 512)), whole((512, 128))],
-        out_specs=[moving] + [whole(s) for s in sums],
-        out_shape=[jax.ShapeDtypeStruct(s, F32) for s in [x.shape] + sums],
+        in_specs=[HBM, HBM] + [VMEM] * 3,
+        out_specs=[HBM] + [VMEM] * 3,
+        out_shape=[jax.ShapeDtypeStruct(x.shape, BF16)]
+        + [jax.ShapeDtypeStruct(s, F32) for s in ((128, 512), (128, 512), (8, 512))],
+        scratch_shapes=[
+            pltpu.VMEM(x.shape, BF16),
+            pltpu.VMEM(c.shape, BF16),
+            pltpu.VMEM(x.shape, BF16),
+            pltpu.SemaphoreType.DMA((3, 4)),
+        ],
         compiler_params=pltpu.CompilerParams(vmem_limit_bytes=52 * MIB),
         cost_estimate=pl.CostEstimate(
-            flops=10 * count * rows * 128 * 512,
-            bytes_accessed=count * rows * 128 * 8,
-            transcendentals=count * rows * 512,
+            flops=10 * rows * 128 * 512, bytes_accessed=rows * 128 * 8, transcendentals=rows * 512
         ),
         name="pointwise",
     )(x, c, up, bias, down)
@@ -208,17 +257,21 @@
                         ]
 
     total = product(basis_ref[...], coef[...], 1, 0)
-    out_ref[0] = (total[:, :128] + p_ref[0]).astype(out_ref.dtype)
-    out_ref[1] = (total[:, 128:] + p_ref[1]).astype(out_ref.dtype)
-
-
-def finish(basis, message, point, rows=1024):
+    out_ref[0] = (total[:, :128] + p_ref[0].astype(F32)).astype(out_ref.dtype)
+    out_ref[1] = (total[:, 128:] + p_ref[1].astype(F32)).astype(out_ref.dtype)
+
+
+def finish(basis, message, point, rows=2048):
     vertices = basis.shape[0]
     both = pl.BlockSpec((2, rows, 128), lambda i: (0, i, 0))
     return pl.pallas_call(
         finish_body,
         grid=(vertices // rows,),
-        in_specs=[pl.BlockSpec((rows, 1024), lambda i: (i, 0)), whole(message.shape), both],
+        in_specs=[
+            pl.BlockSpec((rows, 1024), lambda i: (i, 0)),
+            pl.BlockSpec(message.shape, lambda i: (0, 0, 0)),
+            both,
+        ],
         out_specs=both,
         out_shape=jax.ShapeDtypeStruct((2, vertices, 128), BF16),
         scratch_shapes=[pltpu.VMEM((1024, 256), BF16)],

time: 102 us -> 97.8 us (0.959)
  Pallas kernels: 39.3 us -> 35.1 us
    pallas_call x2, Pallas kernels: 27.8 us -> 24.9 us  [the longest x1 17.2 us: pointwise(): pl.pallas_call(pointwise_body, in_specs=[HBM, HBM] + [VMEM] * 3, out_spec...]
    pallas_call x1, Pallas kernels: 7.66 us -> 6.38 us  [finish(): pl.pallas_call(finish_body, grid=(vertices // rows,), in_specs=[pl.BlockS...]
  transfers between devices with their start and end apart: 13 -> 13, of which waited for: 7 -> 7; matrix products, arithmetic and copies ran while one was open for 2% -> 2% of each run, Pallas kernels for 28% -> 26%
where the time goes in v3:
time: 97.8 us; the launch traced here: 97.3 us
  starting transfers between devices  45.9 us (47%)
  Pallas kernels  35.1 us (36%)
  waiting for transfers between devices  13.6 us (14%)
  matrix products  1.35 us (1%)
    pallas_call x1, Pallas kernels, pointwise(): pl.pallas_call(pointwise_body, in_specs=[HBM, HBM] + [VMEM] * 3, out_spec...  17.2 us
    ppermute x1, starting transfers between devices, per_device(): both = lax.ppermute(samp, SAMP, [(i, 3 - i) for i in range(RING)])  10.1 us
    ppermute x6, starting transfers between devices, shift(): lax.ppermute(value, axis, [(i, (i + by) % RING) for i in range(RING)])  9.17 us
    all_to_all x1, starting transfers between devices, per_device(): messages = lax.all_to_all(packed, ('x', 'y'), 0, 0)  7.73 us
    pallas_call x1, Pallas kernels, project(): pl.pallas_call(project_body, in_specs=[HBM] * 3, out_specs=VMEM, out_shap...  7.71 us
    all_to_all x1, starting transfers between devices, per_device(): message = lax.all_to_all(message, torus, 0, 0)  6.86 us
    all_to_all x1, starting transfers between devices, per_device(): lax.all_to_all(small(pack_body, 'pack', struct((16, 72, 128), BF16), gu,...  6.66 us
    pallas_call x1, Pallas kernels, finish(): pl.pallas_call(finish_body, grid=(vertices // rows,), in_specs=[pl.BlockS...  6.38 us
  transfers between devices with their start and end apart: 13, of which 7 were waited for; matrix products, arithmetic and copies ran while one was open for 2% of the time, Pallas kernels for 26%

profile of v3, /device:TPU:1, one launch (start us, length us, event | category | flops | bytes accessed | tf_op | source)
XLA Modules:
  0.0 97.3 jit_solution(7909770186851280791)
XLA Ops:
  0.6 7.7 %project.1 = bf16[16,64,512]{2,1,0:T(8,128)(2,1)} custom-call(bf16[4096,1024]{1,0:T(8,128)(2,1)} %basis_ref.1, bf16[2,4096,128]{2,1,0:T(8,128)(2,1)} %x_hbm.1, bf16[2,4096,128]{2,1,0:T(8,128)(2,1)} %c_hbm.1), custom_call_target="tpu_custom_call" | custom-call | flops 4294967296 | bytes 13631488 | tf_op jit(solution)/shard_map/project/pallas_call | solution.py:69
  8.3 0.0 copy-start.1
  8.4 0.0 copy-start.2
  8.4 0.0 copy-start.3
  8.4 7.7 %all-to-all-start = ((bf16[16,64,512]{2,1,0:T(8,128)(2,1)}), bf16[16,64,512]{2,1,0:T(8,128)(2,1)S(1)}, u32[]{:S(2)}, u32[]{:S(2)}) async-start(bf16[16,64,512]{2,1,0:T(8,128)(2,1)} %project.1), calls=%async_computation | async-start | bytes 2097152 | tf_op jit(solution)/shard_map/all_to_all | solution.py:308
  16.1 0.0 copy-done.1
  16.1 0.0 copy-done.2
  16.1 0.0 copy-done.3
  16.1 17.2 %pointwise.1 = (bf16[8192,128]{1,0:T(8,128)(2,1)}, f32[128,512]{1,0:T(8,128)S(1)}, f32[128,512]{1,0:T(8,128)S(1)}, f32[8,512]{1,0:T(8,128)S(1)}) custom-call(bf16[8192,128]{1,0:T(8,128)(2,1)} %bitcast.21, bf16[8192,128]{1,0:T(8,128)(2,1)} %bitcast.22, bf16[128,512]{1,0:T(8,128)(2,1)S(1)} %copy-done.1, f32[1,512]{1,0:T(1,128)S(1)} %bitcast.19, ...), custom_call_target="tpu_custom_call" | custom-call | flops 5368709120 | bytes 8388608 | tf_op jit(solution)/shard_map/pointwise/pallas_call | solution.py:144
  33.3 0.0 copy-start
  33.3 0.7 pack.1
  34.1 0.0 all-to-all-done.messages
  34.1 6.7 %all-to-all-start.1 = ((bf16[16,72,128]{2,1,0:T(8,128)(2,1)}), bf16[16,72,128]{2,1,0:T(8,128)(2,1)S(1)}, u32[]{:S(2)}, u32[]{:S(2)}) async-start(bf16[16,72,128]{2,1,0:T(8,128)(2,1)} %pack.1), calls=%async_computation.1 | async-start | bytes 589824 | tf_op jit(solution)/shard_map/all_to_all | solution.py:313
  40.7 0.2 line.1
  40.9 1.7 %collective-permute-start = (f32[16,512]{1,0:T(8,128)S(1)}, f32[16,512]{1,0:T(8,128)S(1)}, u32[]{:S(2)}, u32[]{:S(2)}) collective-permute-start(f32[16,512]{1,0:T(8,128)S(1)} %get-tuple-element.29), channel_id=1, source_target_pairs={{0,4},{4,8},{8,12},{12,0},{1,5},{5,9},{9,13},{13,1},{2,6},{6,10},{... | collective-permute-start | bytes 98312 | tf_op jit(solution)/shard_map/ppermute | solution.py:297
  42.6 3.0 %collective-permute-start.1 = (f32[16,512]{1,0:T(8,128)S(1)}, f32[16,512]{1,0:T(8,128)S(1)}, u32[]{:S(2)}, u32[]{:S(2)}) collective-permute-start(f32[16,512]{1,0:T(8,128)S(1)} %get-tuple-element.30), channel_id=1, source_target_pairs={{0,8},{4,12},{8,0},{12,4},{1,9},{5,13},{9,1},{13,5},{2,10},{6,14},... | collective-permute-start | bytes 98312 | tf_op jit(solution)/shard_map/ppermute | solution.py:297
  45.6 0.7 collective-permute-start.2
  46.4 1.9 %all-to-all-done.1.pieces = bf16[16,72,128]{2,1,0:T(8,128)(2,1)S(1)} async-done(((bf16[16,72,128]{2,1,0:T(8,128)(2,1)}), bf16[16,72,128]{2,1,0:T(8,128)(2,1)S(1)}, u32[]{:S(2)}, u32[]{:S(2)}) %all-to-all-start.1) | async-done | bytes 294944 | tf_op jit(solution)/shard_map/all_to_all | solution.py:313
  48.3 0.0 collective-permute-done.one
  48.3 0.0 collective-permute-done.1.two
  48.3 1.1 %collective-permute-done.2.three = f32[16,512]{1,0:T(8,128)S(1)} collective-permute-done((f32[16,512]{1,0:T(8,128)S(1)}, f32[16,512]{1,0:T(8,128)S(1)}, u32[]{:S(2)}, u32[]{:S(2)}) %collective-permute-start.2) | collective-permute-done | bytes 32800 | tf_op jit(solution)/shard_map/ppermute | solution.py:297
  49.4 0.0 copy-done
  49.4 0.5 own.1
  49.9 3.4 %collective-permute-start.5 = (bf16[104,128]{1,0:T(8,128)(2,1)S(1)}, bf16[104,128]{1,0:T(8,128)(2,1)S(1)}, u32[]{:S(2)}, u32[]{:S(2)}) collective-permute-start(bf16[104,128]{1,0:T(8,128)(2,1)S(1)} %get-tuple-element.37.own), channel_id=1, source_target_pairs={{0,12},{4,0},{8,4},{12,8},{1,13},{5,1},{9,5},{13,9},{2,14},{6,2},{... | collective-permute-start | bytes 79880 | tf_op jit(solution)/shard_map/ppermute | solution.py:297
  53.2 0.0 collective-permute-start.4
  53.2 0.4 collective-permute-start.3
  53.6 0.6 collective-permute-done.5.three
  54.2 2.6 %collective-permute-done.4.two = bf16[104,128]{1,0:T(8,128)(2,1)S(1)} collective-permute-done((bf16[104,128]{1,0:T(8,128)(2,1)S(1)}, bf16[104,128]{1,0:T(8,128)(2,1)S(1)}, u32[]{:S(2)}, u32[]{:S(2)}) %collective-permute-start.4) | collective-permute-done | bytes 26656 | tf_op jit(solution)/shard_map/ppermute | solution.py:297
  56.8 1.2 %collective-permute-done.3.one = bf16[104,128]{1,0:T(8,128)(2,1)S(1)} collective-permute-done((bf16[104,128]{1,0:T(8,128)(2,1)S(1)}, bf16[104,128]{1,0:T(8,128)(2,1)S(1)}, u32[]{:S(2)}, u32[]{:S(2)}) %collective-permute-start.3) | collective-permute-done | bytes 26656 | tf_op jit(solution)/shard_map/ppermute | solution.py:297
  58.0 0.9 gather.1
  58.9 4.8 %all-to-all-start.2 = ((bf16[16,128,128]{2,1,0:T(8,128)(2,1)}), bf16[16,128,128]{2,1,0:T(8,128)(2,1)S(1)}, u32[]{:S(2)}, u32[]{:S(2)}) async-start(bf16[16,128,128]{2,1,0:T(8,128)(2,1)} %get-tuple-element.39), calls=%async_computation.2 | async-start | bytes 1048576 | tf_op jit(solution)/shard_map/all_to_all | solution.py:330
  63.7 10.1 %collective-permute-start.8 = (bf16[136,128]{1,0:T(8,128)(2,1)S(1)}, bf16[136,128]{1,0:T(8,128)(2,1)S(1)}, u32[]{:S(2)}, u32[]{:S(2)}) collective-permute-start(bf16[136,128]{1,0:T(8,128)(2,1)S(1)} %get-tuple-element.40.own), channel_id=1, source_target_pairs={{0,192},{64,128},{128,64},{192,0},{1,193},{65,129},{129,65},{193,1... | collective-permute-start | bytes 104456 | tf_op jit(solution)/shard_map/ppermute | solution.py:333
  73.8 0.3 collective-permute-start.7
  74.1 0.2 collective-permute-start.6
  74.3 1.8 %collective-permute-done.8.both = bf16[136,128]{1,0:T(8,128)(2,1)S(1)} collective-permute-done((bf16[136,128]{1,0:T(8,128)(2,1)S(1)}, bf16[136,128]{1,0:T(8,128)(2,1)S(1)}, u32[]{:S(2)}, u32[]{:S(2)}) %collective-permute-start.8) | collective-permute-done | bytes 34848 | tf_op jit(solution)/shard_map/ppermute | solution.py:333
  76.1 4.4 %collective-permute-done.7.zhi = bf16[136,128]{1,0:T(8,128)(2,1)S(1)} collective-permute-done((bf16[136,128]{1,0:T(8,128)(2,1)S(1)}, bf16[136,128]{1,0:T(8,128)(2,1)S(1)}, u32[]{:S(2)}, u32[]{:S(2)}) %collective-permute-start.7) | collective-permute-done | bytes 34848 | tf_op jit(solution)/shard_map/ppermute | solution.py:332
  80.5 0.0 collective-permute-done.6.core
  80.5 0.7 join.1
  81.2 0.6 slice_bitcast_fusion
  81.8 0.0 all-to-all-done.2.message_ref
  81.8 0.0 copy-start.4
  81.8 6.9 %all-to-all-start.3 = ((bf16[16,64,128]{2,1,0:T(8,128)(2,1)}), bf16[16,64,128]{2,1,0:T(8,128)(2,1)S(1)}, u32[]{:S(2)}, u32[]{:S(2)}) async-start(bf16[16,64,128]{2,1,0:T(8,128)(2,1)} %get-tuple-element.45), calls=%async_computation.3 | async-start | bytes 524288 | tf_op jit(solution)/shard_map/all_to_all | solution.py:340
  88.7 1.3 %convolution_bitcast_fusion = f32[16,128,128]{2,1,0:T(8,128)} fusion(bf16[4,2,1,16,128]{4,3,2,1,0:T(8,128)(2,1)S(1)} %get-tuple-element.50, bf16[4,2,1,16,128]{4,3,2,1,0:T(8,128)(2,1)S(1)} %get-tuple-element.49), kind=kOutput, calls=%fused_computation | convolution fusion | flops 4194304 | bytes 1114112 | tf_op jit(solution)/shard_map/gskc,gskd->kcd/dot_general | solution.py:347
  90.1 0.0 copy-done.4
  90.1 6.4 %finish.1 = bf16[2,4096,128]{2,1,0:T(8,128)(2,1)} custom-call(bf16[4096,1024]{1,0:T(8,128)(2,1)} %basis_ref.1, bf16[16,128,128]{2,1,0:T(8,128)(2,1)} %copy-done.4, bf16[2,4096,128]{2,1,0:T(8,128)(2,1)} %bitcast.20), custom_call_target="tpu_custom_call" | custom-call | flops 2147483648 | bytes 16777216 | tf_op jit(solution)/shard_map/finish/pallas_call | solution.py:267
  96.5 0.0 all-to-all-done.3.message
  96.5 0.8 weights.3
  (1 shorter events, 0.0 us)
Async XLA Ops:
  8.3 7.8 %copy-start.1 = (bf16[128,512]{1,0:T(8,128)(2,1)S(1)}, bf16[128,512]{1,0:T(8,128)(2,1)}, u32[]{:S(2)}) copy-start(bf16[128,512]{1,0:T(8,128)(2,1)} %up_ref.1) | copy-start | bytes 393220
  8.4 7.8 %copy-start.2 = (bf16[512,128]{1,0:T(8,128)(2,1)S(1)}, bf16[512,128]{1,0:T(8,128)(2,1)}, u32[]{:S(2)}) copy-start(bf16[512,128]{1,0:T(8,128)(2,1)} %down_ref.1) | copy-start | bytes 393220
  8.4 7.8 %copy-start.3 = (f32[512]{0:T(512)S(1)}, f32[512]{0:T(512)}, u32[]{:S(2)}) copy-start(f32[512]{0:T(512)} %param.12) | copy-start | bytes 6148
  8.4 25.7 %all-to-all-start = ((bf16[16,64,512]{2,1,0:T(8,128)(2,1)}), bf16[16,64,512]{2,1,0:T(8,128)(2,1)S(1)}, u32[]{:S(2)}, u32[]{:S(2)}) async-start(bf16[16,64,512]{2,1,0:T(8,128)(2,1)} %project.1), calls=%async_computation | async-start | bytes 2097152 | tf_op jit(solution)/shard_map/all_to_all | solution.py:308
  33.3 16.1 %copy-start = (bf16[16,128,128]{2,1,0:T(8,128)(2,1)S(1)}, bf16[16,128,128]{2,1,0:T(8,128)(2,1)}, u32[]{:S(2)}) copy-start(bf16[16,128,128]{2,1,0:T(8,128)(2,1)} %weights.2) | copy-start | bytes 1572868
  34.1 14.2 %all-to-all-start.1 = ((bf16[16,72,128]{2,1,0:T(8,128)(2,1)}), bf16[16,72,128]{2,1,0:T(8,128)(2,1)S(1)}, u32[]{:S(2)}, u32[]{:S(2)}) async-start(bf16[16,72,128]{2,1,0:T(8,128)(2,1)} %pack.1), calls=%async_computation.1 | async-start | bytes 589824 | tf_op jit(solution)/shard_map/all_to_all | solution.py:313
  40.9 7.4 %collective-permute-start = (f32[16,512]{1,0:T(8,128)S(1)}, f32[16,512]{1,0:T(8,128)S(1)}, u32[]{:S(2)}, u32[]{:S(2)}) collective-permute-start(f32[16,512]{1,0:T(8,128)S(1)} %get-tuple-element.29), channel_id=1, source_target_pairs={{0,4},{4,8},{8,12},{12,0},{1,5},{5,9},{9,13},{13,1},{2,6},{6,10},{... | collective-permute-start | bytes 98312 | tf_op jit(solution)/shard_map/ppermute | solution.py:297
  42.6 5.7 %collective-permute-start.1 = (f32[16,512]{1,0:T(8,128)S(1)}, f32[16,512]{1,0:T(8,128)S(1)}, u32[]{:S(2)}, u32[]{:S(2)}) collective-permute-start(f32[16,512]{1,0:T(8,128)S(1)} %get-tuple-element.30), channel_id=1, source_target_pairs={{0,8},{4,12},{8,0},{12,4},{1,9},{5,13},{9,1},{13,5},{2,10},{6,14},... | collective-permute-start | bytes 98312 | tf_op jit(solution)/shard_map/ppermute | solution.py:297
  45.6 3.7 %collective-permute-start.2 = (f32[16,512]{1,0:T(8,128)S(1)}, f32[16,512]{1,0:T(8,128)S(1)}, u32[]{:S(2)}, u32[]{:S(2)}) collective-permute-start(f32[16,512]{1,0:T(8,128)S(1)} %get-tuple-element.31), channel_id=1, source_target_pairs={{0,12},{4,0},{8,4},{12,8},{1,13},{5,1},{9,5},{13,9},{2,14},{6,2},{... | collective-permute-start | bytes 98312 | tf_op jit(solution)/shard_map/ppermute | solution.py:297
  49.9 4.3 %collective-permute-start.5 = (bf16[104,128]{1,0:T(8,128)(2,1)S(1)}, bf16[104,128]{1,0:T(8,128)(2,1)S(1)}, u32[]{:S(2)}, u32[]{:S(2)}) collective-permute-start(bf16[104,128]{1,0:T(8,128)(2,1)S(1)} %get-tuple-element.37.own), channel_id=1, source_target_pairs={{0,12},{4,0},{8,4},{12,8},{1,13},{5,1},{9,5},{13,9},{2,14},{6,2},{... | collective-permute-start | bytes 79880 | tf_op jit(solution)/shard_map/ppermute | solution.py:297
  53.2 3.6 %collective-permute-start.4 = (bf16[104,128]{1,0:T(8,128)(2,1)S(1)}, bf16[104,128]{1,0:T(8,128)(2,1)S(1)}, u32[]{:S(2)}, u32[]{:S(2)}) collective-permute-start(bf16[104,128]{1,0:T(8,128)(2,1)S(1)} %get-tuple-element.37.own), channel_id=1, source_target_pairs={{0,8},{4,12},{8,0},{12,4},{1,9},{5,13},{9,1},{13,5},{2,10},{6,14},... | collective-permute-start | bytes 79880 | tf_op jit(solution)/shard_map/ppermute | solution.py:297
  53.2 4.8 %collective-permute-start.3 = (bf16[104,128]{1,0:T(8,128)(2,1)S(1)}, bf16[104,128]{1,0:T(8,128)(2,1)S(1)}, u32[]{:S(2)}, u32[]{:S(2)}) collective-permute-start(bf16[104,128]{1,0:T(8,128)(2,1)S(1)} %get-tuple-element.37.own), channel_id=1, source_target_pairs={{0,4},{4,8},{8,12},{12,0},{1,5},{5,9},{9,13},{13,1},{2,6},{6,10},{... | collective-permute-start | bytes 79880 | tf_op jit(solution)/shard_map/ppermute | solution.py:297
  58.9 23.0 %all-to-all-start.2 = ((bf16[16,128,128]{2,1,0:T(8,128)(2,1)}), bf16[16,128,128]{2,1,0:T(8,128)(2,1)S(1)}, u32[]{:S(2)}, u32[]{:S(2)}) async-start(bf16[16,128,128]{2,1,0:T(8,128)(2,1)} %get-tuple-element.39), calls=%async_computation.2 | async-start | bytes 1048576 | tf_op jit(solution)/shard_map/all_to_all | solution.py:330
  63.7 12.4 %collective-permute-start.8 = (bf16[136,128]{1,0:T(8,128)(2,1)S(1)}, bf16[136,128]{1,0:T(8,128)(2,1)S(1)}, u32[]{:S(2)}, u32[]{:S(2)}) collective-permute-start(bf16[136,128]{1,0:T(8,128)(2,1)S(1)} %get-tuple-element.40.own), channel_id=1, source_target_pairs={{0,192},{64,128},{128,64},{192,0},{1,193},{65,129},{129,65},{193,1... | collective-permute-start | bytes 104456 | tf_op jit(solution)/shard_map/ppermute | solution.py:333
  73.8 6.7 %collective-permute-start.7 = (bf16[136,128]{1,0:T(8,128)(2,1)S(1)}, bf16[136,128]{1,0:T(8,128)(2,1)S(1)}, u32[]{:S(2)}, u32[]{:S(2)}) collective-permute-start(bf16[136,128]{1,0:T(8,128)(2,1)S(1)} %get-tuple-element.40.own), channel_id=1, source_target_pairs={{0,128},{128,0},{1,129},{129,1},{2,130},{130,2},{3,131},{131,3},{4... | collective-permute-start | bytes 104456 | tf_op jit(solution)/shard_map/ppermute | solution.py:332
  74.1 6.4 %collective-permute-start.6 = (bf16[136,128]{1,0:T(8,128)(2,1)S(1)}, bf16[136,128]{1,0:T(8,128)(2,1)S(1)}, u32[]{:S(2)}, u32[]{:S(2)}) collective-permute-start(bf16[136,128]{1,0:T(8,128)(2,1)S(1)} %get-tuple-element.40.own), channel_id=1, source_target_pairs={{0,64},{64,0},{1,65},{65,1},{2,66},{66,2},{3,67},{67,3},{4,68},{68... | collective-permute-start | bytes 104456 | tf_op jit(solution)/shard_map/ppermute | solution.py:331
  81.8 8.2 %copy-start.4 = (bf16[16,128,128]{2,1,0:T(8,128)(2,1)}, bf16[16,128,128]{2,1,0:T(8,128)(2,1)S(1)}, u32[]{:S(2)}) copy-start(bf16[16,128,128]{2,1,0:T(8,128)(2,1)S(1)} %all-to-all-done.2.message_ref) | copy-start | bytes 1572868
  81.8 14.6 %all-to-all-start.3 = ((bf16[16,64,128]{2,1,0:T(8,128)(2,1)}), bf16[16,64,128]{2,1,0:T(8,128)(2,1)S(1)}, u32[]{:S(2)}, u32[]{:S(2)}) async-start(bf16[16,64,128]{2,1,0:T(8,128)(2,1)} %get-tuple-element.45), calls=%async_computation.3 | async-start | bytes 524288 | tf_op jit(solution)/shard_map/all_to_all | solution.py:340

commit v4 on v3

--- a/solution.py
+++ b/solution.py
@@ -126,13 +126,12 @@
         value = z * q
         hidden = value.astype(BF16)
         slope = q + (value - value * q) * (2.0 * ROOT + (6.0 * CUBE * ROOT) * square)
-        grad_pre = (product(c, down, 1, 1) * slope).astype(BF16)
+        exact = product(c, down, 1, 1) * slope
+        gb_ref[...] += jnp.sum(exact.reshape(rows // 8, 8, 512), axis=0)
+        grad_pre = exact.astype(BF16)
         p_ref[at, :] = product(grad_pre, up, 1, 1).astype(BF16)
         copy(2, i, at).start()
-        with_ones = jnp.concatenate([x, jnp.ones((rows, 128), BF16)], axis=1)
-        sums = product(with_ones, grad_pre, 0, 0)
-        gu_ref[...] += sums[:128]
-        gb_ref[...] += sums[128:136]
+        gu_ref[...] += product(x, grad_pre, 0, 0)
         gd_ref[...] += product(c, hidden, 0, 0)
 
     for i in range(count):
@@ -163,9 +162,10 @@
 
 def pack_body(gu, gd, gb, out):
     row = lax.broadcasted_iota(jnp.int32, (8, 128), 0)
+    sums = jnp.sum(gb[...], axis=0, keepdims=True)
     bias = jnp.zeros((8, 128), F32)
     for g in range(4):
-        bias = jnp.where(row == g, gb[:, g * 128 : (g + 1) * 128], bias)
+        bias = jnp.where(row == g, sums[:, g * 128 : (g + 1) * 128], bias)
     for j in range(16):
         tiles = [
             ref[j * 8 : (j + 1) * 8, g * 128 : (g + 1) * 128] for ref in (gu, gd) for g in range(4)
@@ -233,7 +233,7 @@
     samp_ref[64:136, :] = grads.astype(BF16)
 
 
-def join_body(at, own, core, zhi, both, everyone, bias, message):
+def join_body(at, own, both, zhi, core, everyone, bias, message):
     for mask, ref in enumerate((own, core, zhi, both)):
         everyone[jnp.bitwise_xor(at[0], mask)] = ref[0:64, :]
     parts = [ref[64:136, :].astype(F32) for ref in (own, core, zhi, both)]
@@ -328,13 +328,13 @@
         scratch=[pltpu.VMEM((RING, 32, 128), BF16)],
     )
     coef = lax.all_to_all(coef, torus, 0, 0)
+    both = lax.ppermute(samp, SAMP, [(i, 3 - i) for i in range(RING)])
+    zhi = lax.ppermute(samp, "zhi", [(0, 1), (1, 0)])
     core = lax.ppermute(samp, "core", [(0, 1), (1, 0)])
-    zhi = lax.ppermute(samp, "zhi", [(0, 1), (1, 0)])
-    both = lax.ppermute(samp, SAMP, [(i, 3 - i) for i in range(RING)])
     everyone, bias, message = small(
         join_body, "join",
         [struct((RING, 64, 128), BF16), struct((8, 128), F32), struct((16, 64, 128), BF16)],
-        samp_at, samp, core, zhi, both,
+        samp_at, samp, both, zhi, core,
     )
     coef, message = lax.optimization_barrier((coef, message))
     message = lax.all_to_all(message, torus, 0, 0)

time: 97.8 us -> 98.2 us (level)
    ppermute x1, starting transfers between devices: 10.1 us -> 0.51 us  [per_device(): both = lax.ppermute(samp, SAMP, [(i, 3 - i) for i in range(RING)])]
    ppermute x1, starting transfers between devices: 0.23 us -> 5.15 us  [per_device(): core = lax.ppermute(samp, 'core', [(0, 1), (1, 0)])]
    ppermute x1, starting transfers between devices: 0.26 us -> 5.13 us  [per_device(): zhi = lax.ppermute(samp, 'zhi', [(0, 1), (1, 0)])]
    ppermute x1, waiting for transfers between devices: 1.75 us -> 5.73 us  [per_device(): both = lax.ppermute(samp, SAMP, [(i, 3 - i) for i in range(RING)])]
    ppermute x1, waiting for transfers between devices: 4.44 us -> 1.07 us  [per_device(): zhi = lax.ppermute(samp, 'zhi', [(0, 1), (1, 0)])]
  transfers between devices with their start and end apart: 13 -> 13, of which waited for: 7 -> 7; matrix products, arithmetic and copies ran while one was open for 2% -> 2% of each run, Pallas kernels for 26% -> 25%
where the time goes in v4:
time: 98.2 us; the launch traced here: 97.7 us
  starting transfers between devices  46 us (47%)
  Pallas kernels  34.8 us (35%)
  waiting for transfers between devices  14.2 us (14%)
  matrix products  1.35 us (1%)
    pallas_call x1, Pallas kernels, pointwise(): pl.pallas_call(pointwise_body, in_specs=[HBM, HBM] + [VMEM] * 3, out_spec...  16.9 us
    ppermute x6, starting transfers between devices, shift(): lax.ppermute(value, axis, [(i, (i + by) % RING) for i in range(RING)])  9.18 us
    all_to_all x1, starting transfers between devices, per_device(): messages = lax.all_to_all(packed, ('x', 'y'), 0, 0)  7.73 us
    pallas_call x1, Pallas kernels, project(): pl.pallas_call(project_body, in_specs=[HBM] * 3, out_specs=VMEM, out_shap...  7.71 us
    all_to_all x1, starting transfers between devices, per_device(): message = lax.all_to_all(message, torus, 0, 0)  6.86 us
    all_to_all x1, starting transfers between devices, per_device(): lax.all_to_all(small(pack_body, 'pack', struct((16, 72, 128), BF16), gu,...  6.66 us
    pallas_call x1, Pallas kernels, finish(): pl.pallas_call(finish_body, grid=(vertices // rows,), in_specs=[pl.BlockS...  6.38 us
    ppermute x1, waiting for transfers between devices, per_device(): both = lax.ppermute(samp, SAMP, [(i, 3 - i) for i in range(RING)])  5.73 us
  transfers between devices with their start and end apart: 13, of which 7 were waited for; matrix products, arithmetic and copies ran while one was open for 2% of the time, Pallas kernels for 25%

profile of v4, /device:TPU:1, one launch (start us, length us, event | category | flops | bytes accessed | tf_op | source)
XLA Modules:
  0.0 97.7 jit_solution(6597406496111292865)
XLA Ops:
  0.6 7.7 %project.1 = bf16[16,64,512]{2,1,0:T(8,128)(2,1)} custom-call(bf16[4096,1024]{1,0:T(8,128)(2,1)} %basis_ref.1, bf16[2,4096,128]{2,1,0:T(8,128)(2,1)} %x_hbm.1, bf16[2,4096,128]{2,1,0:T(8,128)(2,1)} %c_hbm.1), custom_call_target="tpu_custom_call" | custom-call | flops 4294967296 | bytes 13631488 | tf_op jit(solution)/shard_map/project/pallas_call | solution.py:69
  8.3 0.0 copy-start.1
  8.4 0.0 copy-start.2
  8.4 0.0 copy-start.3
  8.4 7.7 %all-to-all-start = ((bf16[16,64,512]{2,1,0:T(8,128)(2,1)}), bf16[16,64,512]{2,1,0:T(8,128)(2,1)S(1)}, u32[]{:S(2)}, u32[]{:S(2)}) async-start(bf16[16,64,512]{2,1,0:T(8,128)(2,1)} %project.1), calls=%async_computation | async-start | bytes 2097152 | tf_op jit(solution)/shard_map/all_to_all | solution.py:308
  16.1 0.0 copy-done.1
  16.1 0.0 copy-done.2
  16.1 0.0 copy-done.3
  16.1 16.9 %pointwise.1 = (bf16[8192,128]{1,0:T(8,128)(2,1)}, f32[128,512]{1,0:T(8,128)S(1)}, f32[128,512]{1,0:T(8,128)S(1)}, f32[8,512]{1,0:T(8,128)S(1)}) custom-call(bf16[8192,128]{1,0:T(8,128)(2,1)} %bitcast.21, bf16[8192,128]{1,0:T(8,128)(2,1)} %bitcast.22, bf16[128,512]{1,0:T(8,128)(2,1)S(1)} %copy-done.1, f32[1,512]{1,0:T(1,128)S(1)} %bitcast.19, ...), custom_call_target="tpu_custom_call" | custom-call | flops 5368709120 | bytes 8388608 | tf_op jit(solution)/shard_map/pointwise/pallas_call | solution.py:143
  33.0 0.0 copy-start
  33.0 0.7 pack.1
  33.8 0.0 all-to-all-done.messages
  33.8 6.7 %all-to-all-start.1 = ((bf16[16,72,128]{2,1,0:T(8,128)(2,1)}), bf16[16,72,128]{2,1,0:T(8,128)(2,1)S(1)}, u32[]{:S(2)}, u32[]{:S(2)}) async-start(bf16[16,72,128]{2,1,0:T(8,128)(2,1)} %pack.1), calls=%async_computation.1 | async-start | bytes 589824 | tf_op jit(solution)/shard_map/all_to_all | solution.py:313
  40.5 0.2 line.1
  40.6 1.7 %collective-permute-start = (f32[16,512]{1,0:T(8,128)S(1)}, f32[16,512]{1,0:T(8,128)S(1)}, u32[]{:S(2)}, u32[]{:S(2)}) collective-permute-start(f32[16,512]{1,0:T(8,128)S(1)} %get-tuple-element.29), channel_id=1, source_target_pairs={{0,4},{4,8},{8,12},{12,0},{1,5},{5,9},{9,13},{13,1},{2,6},{6,10},{... | collective-permute-start | bytes 98312 | tf_op jit(solution)/shard_map/ppermute | solution.py:297
  42.3 3.0 %collective-permute-start.1 = (f32[16,512]{1,0:T(8,128)S(1)}, f32[16,512]{1,0:T(8,128)S(1)}, u32[]{:S(2)}, u32[]{:S(2)}) collective-permute-start(f32[16,512]{1,0:T(8,128)S(1)} %get-tuple-element.30), channel_id=1, source_target_pairs={{0,8},{4,12},{8,0},{12,4},{1,9},{5,13},{9,1},{13,5},{2,10},{6,14},... | collective-permute-start | bytes 98312 | tf_op jit(solution)/shard_map/ppermute | solution.py:297
  45.3 0.7 collective-permute-start.2
  46.1 1.9 %all-to-all-done.1.pieces = bf16[16,72,128]{2,1,0:T(8,128)(2,1)S(1)} async-done(((bf16[16,72,128]{2,1,0:T(8,128)(2,1)}), bf16[16,72,128]{2,1,0:T(8,128)(2,1)S(1)}, u32[]{:S(2)}, u32[]{:S(2)}) %all-to-all-start.1) | async-done | bytes 294944 | tf_op jit(solution)/shard_map/all_to_all | solution.py:313
  48.0 0.0 collective-permute-done.one
  48.0 0.0 collective-permute-done.1.two
  48.0 1.1 %collective-permute-done.2.three = f32[16,512]{1,0:T(8,128)S(1)} collective-permute-done((f32[16,512]{1,0:T(8,128)S(1)}, f32[16,512]{1,0:T(8,128)S(1)}, u32[]{:S(2)}, u32[]{:S(2)}) %collective-permute-start.2) | collective-permute-done | bytes 32800 | tf_op jit(solution)/shard_map/ppermute | solution.py:297
  49.1 0.0 copy-done
  49.1 0.5 own.1
  49.6 3.4 %collective-permute-start.5 = (bf16[104,128]{1,0:T(8,128)(2,1)S(1)}, bf16[104,128]{1,0:T(8,128)(2,1)S(1)}, u32[]{:S(2)}, u32[]{:S(2)}) collective-permute-start(bf16[104,128]{1,0:T(8,128)(2,1)S(1)} %get-tuple-element.37.own), channel_id=1, source_target_pairs={{0,12},{4,0},{8,4},{12,8},{1,13},{5,1},{9,5},{13,9},{2,14},{6,2},{... | collective-permute-start | bytes 79880 | tf_op jit(solution)/shard_map/ppermute | solution.py:297
  52.9 0.0 collective-permute-start.4
  52.9 0.4 collective-permute-start.3
  53.3 0.6 collective-permute-done.5.three
  53.9 2.6 %collective-permute-done.4.two = bf16[104,128]{1,0:T(8,128)(2,1)S(1)} collective-permute-done((bf16[104,128]{1,0:T(8,128)(2,1)S(1)}, bf16[104,128]{1,0:T(8,128)(2,1)S(1)}, u32[]{:S(2)}, u32[]{:S(2)}) %collective-permute-start.4) | collective-permute-done | bytes 26656 | tf_op jit(solution)/shard_map/ppermute | solution.py:297
  56.5 1.2 %collective-permute-done.3.one = bf16[104,128]{1,0:T(8,128)(2,1)S(1)} collective-permute-done((bf16[104,128]{1,0:T(8,128)(2,1)S(1)}, bf16[104,128]{1,0:T(8,128)(2,1)S(1)}, u32[]{:S(2)}, u32[]{:S(2)}) %collective-permute-start.3) | collective-permute-done | bytes 26656 | tf_op jit(solution)/shard_map/ppermute | solution.py:297
  57.7 0.9 gather.1
  58.6 4.8 %all-to-all-start.2 = ((bf16[16,128,128]{2,1,0:T(8,128)(2,1)}), bf16[16,128,128]{2,1,0:T(8,128)(2,1)S(1)}, u32[]{:S(2)}, u32[]{:S(2)}) async-start(bf16[16,128,128]{2,1,0:T(8,128)(2,1)} %get-tuple-element.39), calls=%async_computation.2 | async-start | bytes 1048576 | tf_op jit(solution)/shard_map/all_to_all | solution.py:330
  63.4 5.1 %collective-permute-start.8 = (bf16[136,128]{1,0:T(8,128)(2,1)S(1)}, bf16[136,128]{1,0:T(8,128)(2,1)S(1)}, u32[]{:S(2)}, u32[]{:S(2)}) collective-permute-start(bf16[136,128]{1,0:T(8,128)(2,1)S(1)} %get-tuple-element.40.own), channel_id=1, source_target_pairs={{0,64},{64,0},{1,65},{65,1},{2,66},{66,2},{3,67},{67,3},{4,68},{68... | collective-permute-start | bytes 104456 | tf_op jit(solution)/shard_map/ppermute | solution.py:333
  68.5 5.1 %collective-permute-start.7 = (bf16[136,128]{1,0:T(8,128)(2,1)S(1)}, bf16[136,128]{1,0:T(8,128)(2,1)S(1)}, u32[]{:S(2)}, u32[]{:S(2)}) collective-permute-start(bf16[136,128]{1,0:T(8,128)(2,1)S(1)} %get-tuple-element.40.own), channel_id=1, source_target_pairs={{0,128},{128,0},{1,129},{129,1},{2,130},{130,2},{3,131},{131,3},{4... | collective-permute-start | bytes 104456 | tf_op jit(solution)/shard_map/ppermute | solution.py:332
  73.7 0.5 collective-permute-start.6
  74.2 0.0 collective-permute-done.8.core
  74.2 1.1 %collective-permute-done.7.zhi = bf16[136,128]{1,0:T(8,128)(2,1)S(1)} collective-permute-done((bf16[136,128]{1,0:T(8,128)(2,1)S(1)}, bf16[136,128]{1,0:T(8,128)(2,1)S(1)}, u32[]{:S(2)}, u32[]{:S(2)}) %collective-permute-start.7) | collective-permute-done | bytes 34848 | tf_op jit(solution)/shard_map/ppermute | solution.py:332
  75.2 5.7 %collective-permute-done.6.both = bf16[136,128]{1,0:T(8,128)(2,1)S(1)} collective-permute-done((bf16[136,128]{1,0:T(8,128)(2,1)S(1)}, bf16[136,128]{1,0:T(8,128)(2,1)S(1)}, u32[]{:S(2)}, u32[]{:S(2)}) %collective-permute-start.6) | collective-permute-done | bytes 34848 | tf_op jit(solution)/shard_map/ppermute | solution.py:331
  81.0 0.7 join.1
  81.7 0.6 slice_bitcast_fusion
  82.3 0.0 all-to-all-done.2.message_ref
  82.3 0.0 copy-start.4
  82.3 6.9 %all-to-all-start.3 = ((bf16[16,64,128]{2,1,0:T(8,128)(2,1)}), bf16[16,64,128]{2,1,0:T(8,128)(2,1)S(1)}, u32[]{:S(2)}, u32[]{:S(2)}) async-start(bf16[16,64,128]{2,1,0:T(8,128)(2,1)} %get-tuple-element.45), calls=%async_computation.3 | async-start | bytes 524288 | tf_op jit(solution)/shard_map/all_to_all | solution.py:340
  89.2 1.3 %convolution_bitcast_fusion = f32[16,128,128]{2,1,0:T(8,128)} fusion(bf16[4,2,1,16,128]{4,3,2,1,0:T(8,128)(2,1)S(1)} %get-tuple-element.50, bf16[4,2,1,16,128]{4,3,2,1,0:T(8,128)(2,1)S(1)} %get-tuple-element.49), kind=kOutput, calls=%fused_computation | convolution fusion | flops 4194304 | bytes 1114112 | tf_op jit(solution)/shard_map/gskc,gskd->kcd/dot_general | solution.py:347
  90.5 0.0 copy-done.4
  90.5 6.4 %finish.1 = bf16[2,4096,128]{2,1,0:T(8,128)(2,1)} custom-call(bf16[4096,1024]{1,0:T(8,128)(2,1)} %basis_ref.1, bf16[16,128,128]{2,1,0:T(8,128)(2,1)} %copy-done.4, bf16[2,4096,128]{2,1,0:T(8,128)(2,1)} %bitcast.20), custom_call_target="tpu_custom_call" | custom-call | flops 2147483648 | bytes 16777216 | tf_op jit(solution)/shard_map/finish/pallas_call | solution.py:267
  96.9 0.0 all-to-all-done.3.message
  96.9 0.8 weights.3
  (1 shorter events, 0.0 us)
Async XLA Ops:
  8.3 7.8 %copy-start.1 = (bf16[128,512]{1,0:T(8,128)(2,1)S(1)}, bf16[128,512]{1,0:T(8,128)(2,1)}, u32[]{:S(2)}) copy-start(bf16[128,512]{1,0:T(8,128)(2,1)} %up_ref.1) | copy-start | bytes 393220
  8.4 7.8 %copy-start.2 = (bf16[512,128]{1,0:T(8,128)(2,1)S(1)}, bf16[512,128]{1,0:T(8,128)(2,1)}, u32[]{:S(2)}) copy-start(bf16[512,128]{1,0:T(8,128)(2,1)} %down_ref.1) | copy-start | bytes 393220
  8.4 7.8 %copy-start.3 = (f32[512]{0:T(512)S(1)}, f32[512]{0:T(512)}, u32[]{:S(2)}) copy-start(f32[512]{0:T(512)} %param.12) | copy-start | bytes 6148
  8.4 25.4 %all-to-all-start = ((bf16[16,64,512]{2,1,0:T(8,128)(2,1)}), bf16[16,64,512]{2,1,0:T(8,128)(2,1)S(1)}, u32[]{:S(2)}, u32[]{:S(2)}) async-start(bf16[16,64,512]{2,1,0:T(8,128)(2,1)} %project.1), calls=%async_computation | async-start | bytes 2097152 | tf_op jit(solution)/shard_map/all_to_all | solution.py:308
  33.0 16.1 %copy-start = (bf16[16,128,128]{2,1,0:T(8,128)(2,1)S(1)}, bf16[16,128,128]{2,1,0:T(8,128)(2,1)}, u32[]{:S(2)}) copy-start(bf16[16,128,128]{2,1,0:T(8,128)(2,1)} %weights.2) | copy-start | bytes 1572868
  33.8 14.2 %all-to-all-start.1 = ((bf16[16,72,128]{2,1,0:T(8,128)(2,1)}), bf16[16,72,128]{2,1,0:T(8,128)(2,1)S(1)}, u32[]{:S(2)}, u32[]{:S(2)}) async-start(bf16[16,72,128]{2,1,0:T(8,128)(2,1)} %pack.1), calls=%async_computation.1 | async-start | bytes 589824 | tf_op jit(solution)/shard_map/all_to_all | solution.py:313
  40.6 7.4 %collective-permute-start = (f32[16,512]{1,0:T(8,128)S(1)}, f32[16,512]{1,0:T(8,128)S(1)}, u32[]{:S(2)}, u32[]{:S(2)}) collective-permute-start(f32[16,512]{1,0:T(8,128)S(1)} %get-tuple-element.29), channel_id=1, source_target_pairs={{0,4},{4,8},{8,12},{12,0},{1,5},{5,9},{9,13},{13,1},{2,6},{6,10},{... | collective-permute-start | bytes 98312 | tf_op jit(solution)/shard_map/ppermute | solution.py:297
  42.3 5.7 %collective-permute-start.1 = (f32[16,512]{1,0:T(8,128)S(1)}, f32[16,512]{1,0:T(8,128)S(1)}, u32[]{:S(2)}, u32[]{:S(2)}) collective-permute-start(f32[16,512]{1,0:T(8,128)S(1)} %get-tuple-element.30), channel_id=1, source_target_pairs={{0,8},{4,12},{8,0},{12,4},{1,9},{5,13},{9,1},{13,5},{2,10},{6,14},... | collective-permute-start | bytes 98312 | tf_op jit(solution)/shard_map/ppermute | solution.py:297
  45.3 3.7 %collective-permute-start.2 = (f32[16,512]{1,0:T(8,128)S(1)}, f32[16,512]{1,0:T(8,128)S(1)}, u32[]{:S(2)}, u32[]{:S(2)}) collective-permute-start(f32[16,512]{1,0:T(8,128)S(1)} %get-tuple-element.31), channel_id=1, source_target_pairs={{0,12},{4,0},{8,4},{12,8},{1,13},{5,1},{9,5},{13,9},{2,14},{6,2},{... | collective-permute-start | bytes 98312 | tf_op jit(solution)/shard_map/ppermute | solution.py:297
  49.6 4.3 %collective-permute-start.5 = (bf16[104,128]{1,0:T(8,128)(2,1)S(1)}, bf16[104,128]{1,0:T(8,128)(2,1)S(1)}, u32[]{:S(2)}, u32[]{:S(2)}) collective-permute-start(bf16[104,128]{1,0:T(8,128)(2,1)S(1)} %get-tuple-element.37.own), channel_id=1, source_target_pairs={{0,12},{4,0},{8,4},{12,8},{1,13},{5,1},{9,5},{13,9},{2,14},{6,2},{... | collective-permute-start | bytes 79880 | tf_op jit(solution)/shard_map/ppermute | solution.py:297
  52.9 3.6 %collective-permute-start.4 = (bf16[104,128]{1,0:T(8,128)(2,1)S(1)}, bf16[104,128]{1,0:T(8,128)(2,1)S(1)}, u32[]{:S(2)}, u32[]{:S(2)}) collective-permute-start(bf16[104,128]{1,0:T(8,128)(2,1)S(1)} %get-tuple-element.37.own), channel_id=1, source_target_pairs={{0,8},{4,12},{8,0},{12,4},{1,9},{5,13},{9,1},{13,5},{2,10},{6,14},... | collective-permute-start | bytes 79880 | tf_op jit(solution)/shard_map/ppermute | solution.py:297
  52.9 4.8 %collective-permute-start.3 = (bf16[104,128]{1,0:T(8,128)(2,1)S(1)}, bf16[104,128]{1,0:T(8,128)(2,1)S(1)}, u32[]{:S(2)}, u32[]{:S(2)}) collective-permute-start(bf16[104,128]{1,0:T(8,128)(2,1)S(1)} %get-tuple-element.37.own), channel_id=1, source_target_pairs={{0,4},{4,8},{8,12},{12,0},{1,5},{5,9},{9,13},{13,1},{2,6},{6,10},{... | collective-permute-start | bytes 79880 | tf_op jit(solution)/shard_map/ppermute | solution.py:297
  58.6 23.7 %all-to-all-start.2 = ((bf16[16,128,128]{2,1,0:T(8,128)(2,1)}), bf16[16,128,128]{2,1,0:T(8,128)(2,1)S(1)}, u32[]{:S(2)}, u32[]{:S(2)}) async-start(bf16[16,128,128]{2,1,0:T(8,128)(2,1)} %get-tuple-element.39), calls=%async_computation.2 | async-start | bytes 1048576 | tf_op jit(solution)/shard_map/all_to_all | solution.py:330
  63.4 10.8 %collective-permute-start.8 = (bf16[136,128]{1,0:T(8,128)(2,1)S(1)}, bf16[136,128]{1,0:T(8,128)(2,1)S(1)}, u32[]{:S(2)}, u32[]{:S(2)}) collective-permute-start(bf16[136,128]{1,0:T(8,128)(2,1)S(1)} %get-tuple-element.40.own), channel_id=1, source_target_pairs={{0,64},{64,0},{1,65},{65,1},{2,66},{66,2},{3,67},{67,3},{4,68},{68... | collective-permute-start | bytes 104456 | tf_op jit(solution)/shard_map/ppermute | solution.py:333
  68.5 6.7 %collective-permute-start.7 = (bf16[136,128]{1,0:T(8,128)(2,1)S(1)}, bf16[136,128]{1,0:T(8,128)(2,1)S(1)}, u32[]{:S(2)}, u32[]{:S(2)}) collective-permute-start(bf16[136,128]{1,0:T(8,128)(2,1)S(1)} %get-tuple-element.40.own), channel_id=1, source_target_pairs={{0,128},{128,0},{1,129},{129,1},{2,130},{130,2},{3,131},{131,3},{4... | collective-permute-start | bytes 104456 | tf_op jit(solution)/shard_map/ppermute | solution.py:332
  73.7 7.3 %collective-permute-start.6 = (bf16[136,128]{1,0:T(8,128)(2,1)S(1)}, bf16[136,128]{1,0:T(8,128)(2,1)S(1)}, u32[]{:S(2)}, u32[]{:S(2)}) collective-permute-start(bf16[136,128]{1,0:T(8,128)(2,1)S(1)} %get-tuple-element.40.own), channel_id=1, source_target_pairs={{0,192},{64,128},{128,64},{192,0},{1,193},{65,129},{129,65},{193,1... | collective-permute-start | bytes 104456 | tf_op jit(solution)/shard_map/ppermute | solution.py:331
  82.3 8.2 %copy-start.4 = (bf16[16,128,128]{2,1,0:T(8,128)(2,1)}, bf16[16,128,128]{2,1,0:T(8,128)(2,1)S(1)}, u32[]{:S(2)}) copy-start(bf16[16,128,128]{2,1,0:T(8,128)(2,1)S(1)} %all-to-all-done.2.message_ref) | copy-start | bytes 1572868
  82.3 14.6 %all-to-all-start.3 = ((bf16[16,64,128]{2,1,0:T(8,128)(2,1)}), bf16[16,64,128]{2,1,0:T(8,128)(2,1)S(1)}, u32[]{:S(2)}, u32[]{:S(2)}) async-start(bf16[16,64,128]{2,1,0:T(8,128)(2,1)} %get-tuple-element.45), calls=%async_computation.3 | async-start | bytes 524288 | tf_op jit(solution)/shard_map/all_to_all | solution.py:340

commit v5 on v4

--- a/solution.py
+++ b/solution.py
@@ -25,6 +25,7 @@
 
 PIECES = 8
 AHEAD = 3
+STEP = 2048
 VMEM = pl.BlockSpec(memory_space=pltpu.VMEM)
 HBM = pl.BlockSpec(memory_space=pltpu.HBM)
 
@@ -87,9 +88,9 @@
 
 
 def pointwise_body(
-    x_hbm, c_hbm, up_ref, bias_ref, down_ref, p_hbm, gu_ref, gd_ref, gb_ref, x_ref, c_ref, p_ref, sems
+    x_hbm, c_hbm, up_ref, bias_ref, down_ref, p_hbm, out, x_ref, c_ref, p_ref, gu_ref, gd_ref, gb_ref, sems
 ):
-    rows = 2048
+    rows = STEP
     count = x_ref.shape[0] // rows
 
     def copy(k, i, at):
@@ -134,6 +135,18 @@
         gu_ref[...] += product(x, grad_pre, 0, 0)
         gd_ref[...] += product(c, hidden, 0, 0)
 
+    row = lax.broadcasted_iota(jnp.int32, (8, 128), 0)
+    sums = jnp.sum(gb_ref[...], axis=0, keepdims=True)
+    bias = jnp.zeros((8, 128), F32)
+    for g in range(4):
+        bias = jnp.where(row == g, sums[:, g * 128 : (g + 1) * 128], bias)
+    for j in range(16):
+        tiles = [
+            ref[j * 8 : (j + 1) * 8, g * 128 : (g + 1) * 128]
+            for ref in (gu_ref, gd_ref)
+            for g in range(4)
+        ]
+        out[j] = jnp.concatenate(tiles + [bias], axis=0).astype(BF16)
     for i in range(count):
         copy(2, i, pl.ds(i * rows, rows)).wait()
 
@@ -143,14 +156,14 @@
     return pl.pallas_call(
         pointwise_body,
         in_specs=[HBM, HBM] + [VMEM] * 3,
-        out_specs=[HBM] + [VMEM] * 3,
-        out_shape=[jax.ShapeDtypeStruct(x.shape, BF16)]
-        + [jax.ShapeDtypeStruct(s, F32) for s in ((128, 512), (128, 512), (8, 512))],
+        out_specs=[HBM, VMEM],
+        out_shape=[jax.ShapeDtypeStruct(s, BF16) for s in (x.shape, (16, 72, 128))],
         scratch_shapes=[
             pltpu.VMEM(x.shape, BF16),
             pltpu.VMEM(c.shape, BF16),
             pltpu.VMEM(x.shape, BF16),
-            pltpu.SemaphoreType.DMA((3, 4)),
+            *[pltpu.VMEM(s, F32) for s in ((128, 512), (128, 512), (8, 512))],
+            pltpu.SemaphoreType.DMA((3, rows // STEP)),
         ],
         compiler_params=pltpu.CompilerParams(vmem_limit_bytes=52 * MIB),
         cost_estimate=pl.CostEstimate(
@@ -158,19 +171,6 @@
         ),
         name="pointwise",
     )(x, c, up, bias, down)
-
-
-def pack_body(gu, gd, gb, out):
-    row = lax.broadcasted_iota(jnp.int32, (8, 128), 0)
-    sums = jnp.sum(gb[...], axis=0, keepdims=True)
-    bias = jnp.zeros((8, 128), F32)
-    for g in range(4):
-        bias = jnp.where(row == g, sums[:, g * 128 : (g + 1) * 128], bias)
-    for j in range(16):
-        tiles = [
-            ref[j * 8 : (j + 1) * 8, g * 128 : (g + 1) * 128] for ref in (gu, gd) for g in range(4)
-        ]
-        out[j] = jnp.concatenate(tiles + [bias], axis=0).astype(BF16)
 
 
 def small(body, name, out_shape, *args, scratch=()):
@@ -233,12 +233,20 @@
     samp_ref[64:136, :] = grads.astype(BF16)
 
 
-def join_body(at, own, both, zhi, core, everyone, bias, message):
-    for mask, ref in enumerate((own, core, zhi, both)):
-        everyone[jnp.bitwise_xor(at[0], mask)] = ref[0:64, :]
-    parts = [ref[64:136, :].astype(F32) for ref in (own, core, zhi, both)]
-    grads = (parts[0] + parts[1]) + (parts[2] + parts[3])
-    bias[...] = grads[64:72]
+def pair_body(at, own, core, out):
+    place = lax.rem(at[0], 2)
+    for k, ref in ((place, own), (1 - place, core)):
+        out[pl.ds(pl.multiple_of(k * 64, 64), 64), :] = ref[0:64, :]
+    grads = own[64:136, :].astype(F32) + core[64:136, :].astype(F32)
+    out[128:200, :] = grads.astype(BF16)
+
+
+def join_body(at, own, zhi, everyone, bias, message):
+    half = lax.div(at[0], 2)
+    everyone[half] = own[0:128, :]
+    everyone[1 - half] = zhi[0:128, :]
+    grads = own[128:200, :].astype(F32) + zhi[128:200, :].astype(F32)
+    bias[...] = jnp.concatenate([grads[64 + g : 65 + g] for g in range(4)], axis=1)
     body = grads[0:64].astype(BF16)
     for v in range(16):
         message[v] = body
@@ -306,13 +314,11 @@
     packed = project(basis, inputs, cotangent)
     inputs, cotangent, packed = lax.optimization_barrier((inputs, cotangent, packed))
     messages = lax.all_to_all(packed, ("x", "y"), 0, 0)
-    point, gu, gd, gb = pointwise(
+    point, pieces = pointwise(
         inputs.reshape(-1, 128), cotangent.reshape(-1, 128), w_up, b_up.reshape(1, 512), w_down
     )
     torus = ("x", "y")
-    pieces = lax.all_to_all(
-        small(pack_body, "pack", struct((16, 72, 128), BF16), gu, gd, gb), torus, 0, 0
-    )
+    pieces = lax.all_to_all(pieces, torus, 0, 0)
     own, *chunks = small(
         line_body, "line", [struct((16, 512), F32)] * 4,
         z_at, messages, scratch=[pltpu.VMEM((64, 512), F32)],
@@ -328,13 +334,13 @@
         scratch=[pltpu.VMEM((RING, 32, 128), BF16)],
     )
     coef = lax.all_to_all(coef, torus, 0, 0)
-    both = lax.ppermute(samp, SAMP, [(i, 3 - i) for i in range(RING)])
-    zhi = lax.ppermute(samp, "zhi", [(0, 1), (1, 0)])
     core = lax.ppermute(samp, "core", [(0, 1), (1, 0)])
+    pair = small(pair_body, "pair", struct((200, 128), BF16), samp_at, samp, core)
+    zhi = lax.ppermute(pair, "zhi", [(0, 1), (1, 0)])
     everyone, bias, message = small(
         join_body, "join",
-        [struct((RING, 64, 128), BF16), struct((8, 128), F32), struct((16, 64, 128), BF16)],
-        samp_at, samp, both, zhi, core,
+        [struct((2, 128, 128), BF16), struct((1, 512), F32), struct((16, 64, 128), BF16)],
+        samp_at, pair, zhi,
     )
     coef, message = lax.optimization_barrier((coef, message))
     message = lax.all_to_all(message, torus, 0, 0)
@@ -347,7 +353,7 @@
     grad_modes = jnp.einsum(
         "gskc,gskd->kcd", everyone[:, :, 0], everyone[:, :, 1], preferred_element_type=F32
     )
-    return (grad_input, grad_modes, grad_w_up, bias[:4].reshape(512), grad_w_down)
+    return (grad_input, grad_modes, grad_w_up, bias.reshape(512), grad_w_down)
 
 
 def solution(mesh):

time: 98.2 us -> 93.8 us (0.955)
  waiting for transfers between devices: 14.2 us -> 10.1 us
    ppermute x2 -> x1, waiting for transfers between devices: 6.8 us -> 1.86 us  [per_device(): zhi = lax.ppermute(pair, 'zhi', [(0, 1), (1, 0)])]
    ppermute x2 -> x1, starting transfers between devices: 5.64 us -> 5.2 us  [per_device(): zhi = lax.ppermute(pair, 'zhi', [(0, 1), (1, 0)])]
  transfers between devices with their start and end apart: 13 -> 12, of which waited for: 7 -> 7; matrix products, arithmetic and copies ran while one was open for 2% -> 1% of each run, Pallas kernels for 25% -> 27%
where the time goes in v5:
time: 93.8 us; the launch traced here: 92.7 us
  starting transfers between devices  45.6 us (49%)
  Pallas kernels  34.8 us (37%)
  waiting for transfers between devices  10.1 us (11%)
  matrix products  1.35 us (1%)
    pallas_call x1, Pallas kernels, pointwise(): pl.pallas_call(pointwise_body, in_specs=[HBM, HBM] + [VMEM] * 3, out_spec...  17.6 us
    ppermute x6, starting transfers between devices, shift(): lax.ppermute(value, axis, [(i, (i + by) % RING) for i in range(RING)])  9.16 us
    all_to_all x1, starting transfers between devices, per_device(): messages = lax.all_to_all(packed, ('x', 'y'), 0, 0)  7.73 us
    pallas_call x1, Pallas kernels, project(): pl.pallas_call(project_body, in_specs=[HBM] * 3, out_specs=VMEM, out_shap...  7.71 us
    all_to_all x1, starting transfers between devices, per_device(): message = lax.all_to_all(message, torus, 0, 0)  6.86 us
    all_to_all x1, starting transfers between devices, per_device(): pieces = lax.all_to_all(pieces, torus, 0, 0)  6.66 us
    pallas_call x1, Pallas kernels, finish(): pl.pallas_call(finish_body, grid=(vertices // rows,), in_specs=[pl.BlockS...  6.38 us
    ppermute x6, waiting for transfers between devices, shift(): lax.ppermute(value, axis, [(i, (i + by) % RING) for i in range(RING)])  5.45 us
  transfers between devices with their start and end apart: 12, of which 7 were waited for; matrix products, arithmetic and copies ran while one was open for 1% of the time, Pallas kernels for 27%

profile of v5, /device:TPU:1, one launch (start us, length us, event | category | flops | bytes accessed | tf_op | source)
XLA Modules:
  0.0 92.7 jit_solution(13876739933727784850)
XLA Ops:
  0.6 7.7 %project.1 = bf16[16,64,512]{2,1,0:T(8,128)(2,1)} custom-call(bf16[4096,1024]{1,0:T(8,128)(2,1)} %basis_ref.1, bf16[2,4096,128]{2,1,0:T(8,128)(2,1)} %x_hbm.1, bf16[2,4096,128]{2,1,0:T(8,128)(2,1)} %c_hbm.1), custom_call_target="tpu_custom_call" | custom-call | flops 4294967296 | bytes 13631488 | tf_op jit(solution)/shard_map/project/pallas_call | solution.py:70
  8.3 0.0 copy-start.1
  8.4 0.0 copy-start.2
  8.4 0.0 copy-start.3
  8.4 7.7 %all-to-all-start = ((bf16[16,64,512]{2,1,0:T(8,128)(2,1)}), bf16[16,64,512]{2,1,0:T(8,128)(2,1)S(1)}, u32[]{:S(2)}, u32[]{:S(2)}) async-start(bf16[16,64,512]{2,1,0:T(8,128)(2,1)} %project.1), calls=%async_computation | async-start | bytes 2097152 | tf_op jit(solution)/shard_map/all_to_all | solution.py:316
  16.1 0.0 copy-done.1
  16.1 0.0 copy-done.2
  16.1 0.0 copy-done.3
  16.1 0.0 copy-start
  16.2 17.6 %pointwise.1 = (bf16[8192,128]{1,0:T(8,128)(2,1)}, bf16[16,72,128]{2,1,0:T(8,128)(2,1)}) custom-call(bf16[8192,128]{1,0:T(8,128)(2,1)} %bitcast.20, bf16[8192,128]{1,0:T(8,128)(2,1)} %bitcast.21, bf16[128,512]{1,0:T(8,128)(2,1)S(1)} %copy-done.1, f32[1,512]{1,0:T(1,128)S(1)} %bitcast.18, bf16[512,128]{1,0:T(8,128)(2,1)S(1)} %copy-done.2), custom_call_target="tpu_custom_call" | custom-call | flops 5368709120 | bytes 8388608 | tf_op jit(solution)/shard_map/pointwise/pallas_call | solution.py:156
  33.8 0.0 all-to-all-done.messages
  33.8 6.7 %all-to-all-start.1 = ((bf16[16,72,128]{2,1,0:T(8,128)(2,1)}), bf16[16,72,128]{2,1,0:T(8,128)(2,1)S(1)}, u32[]{:S(2)}, u32[]{:S(2)}) async-start(bf16[16,72,128]{2,1,0:T(8,128)(2,1)} %get-tuple-element.32), calls=%async_computation.1 | async-start | bytes 589824 | tf_op jit(solution)/shard_map/all_to_all | solution.py:321
  40.5 0.2 line.1
  40.7 1.7 %collective-permute-start = (f32[16,512]{1,0:T(8,128)S(1)}, f32[16,512]{1,0:T(8,128)S(1)}, u32[]{:S(2)}, u32[]{:S(2)}) collective-permute-start(f32[16,512]{1,0:T(8,128)S(1)} %get-tuple-element.27), channel_id=1, source_target_pairs={{0,4},{4,8},{8,12},{12,0},{1,5},{5,9},{9,13},{13,1},{2,6},{6,10},{... | collective-permute-start | bytes 98312 | tf_op jit(solution)/shard_map/ppermute | solution.py:305
  42.4 3.0 %collective-permute-start.1 = (f32[16,512]{1,0:T(8,128)S(1)}, f32[16,512]{1,0:T(8,128)S(1)}, u32[]{:S(2)}, u32[]{:S(2)}) collective-permute-start(f32[16,512]{1,0:T(8,128)S(1)} %get-tuple-element.28), channel_id=1, source_target_pairs={{0,8},{4,12},{8,0},{12,4},{1,9},{5,13},{9,1},{13,5},{2,10},{6,14},... | collective-permute-start | bytes 98312 | tf_op jit(solution)/shard_map/ppermute | solution.py:305
  45.4 0.7 collective-permute-start.2
  46.1 1.9 %all-to-all-done.1.pieces = bf16[16,72,128]{2,1,0:T(8,128)(2,1)S(1)} async-done(((bf16[16,72,128]{2,1,0:T(8,128)(2,1)}), bf16[16,72,128]{2,1,0:T(8,128)(2,1)S(1)}, u32[]{:S(2)}, u32[]{:S(2)}) %all-to-all-start.1) | async-done | bytes 294944 | tf_op jit(solution)/shard_map/all_to_all | solution.py:321
  48.0 0.0 collective-permute-done.one
  48.1 0.0 collective-permute-done.1.two
  48.1 1.1 %collective-permute-done.2.three = f32[16,512]{1,0:T(8,128)S(1)} collective-permute-done((f32[16,512]{1,0:T(8,128)S(1)}, f32[16,512]{1,0:T(8,128)S(1)}, u32[]{:S(2)}, u32[]{:S(2)}) %collective-permute-start.2) | collective-permute-done | bytes 32800 | tf_op jit(solution)/shard_map/ppermute | solution.py:305
  49.1 0.0 copy-done
  49.1 0.5 own.1
  49.6 3.4 %collective-permute-start.5 = (bf16[104,128]{1,0:T(8,128)(2,1)S(1)}, bf16[104,128]{1,0:T(8,128)(2,1)S(1)}, u32[]{:S(2)}, u32[]{:S(2)}) collective-permute-start(bf16[104,128]{1,0:T(8,128)(2,1)S(1)} %get-tuple-element.33.own), channel_id=1, source_target_pairs={{0,12},{4,0},{8,4},{12,8},{1,13},{5,1},{9,5},{13,9},{2,14},{6,2},{... | collective-permute-start | bytes 79880 | tf_op jit(solution)/shard_map/ppermute | solution.py:305
  53.0 0.0 collective-permute-start.4
  53.0 0.4 collective-permute-start.3
  53.4 0.6 collective-permute-done.5.three
  53.9 2.6 %collective-permute-done.4.two = bf16[104,128]{1,0:T(8,128)(2,1)S(1)} collective-permute-done((bf16[104,128]{1,0:T(8,128)(2,1)S(1)}, bf16[104,128]{1,0:T(8,128)(2,1)S(1)}, u32[]{:S(2)}, u32[]{:S(2)}) %collective-permute-start.4) | collective-permute-done | bytes 26656 | tf_op jit(solution)/shard_map/ppermute | solution.py:305
  56.6 1.2 %collective-permute-done.3.one = bf16[104,128]{1,0:T(8,128)(2,1)S(1)} collective-permute-done((bf16[104,128]{1,0:T(8,128)(2,1)S(1)}, bf16[104,128]{1,0:T(8,128)(2,1)S(1)}, u32[]{:S(2)}, u32[]{:S(2)}) %collective-permute-start.3) | collective-permute-done | bytes 26656 | tf_op jit(solution)/shard_map/ppermute | solution.py:305
  57.7 0.9 gather.1
  58.6 4.8 %all-to-all-start.2 = ((bf16[16,128,128]{2,1,0:T(8,128)(2,1)}), bf16[16,128,128]{2,1,0:T(8,128)(2,1)S(1)}, u32[]{:S(2)}, u32[]{:S(2)}) async-start(bf16[16,128,128]{2,1,0:T(8,128)(2,1)} %get-tuple-element.35), calls=%async_computation.2 | async-start | bytes 1048576 | tf_op jit(solution)/shard_map/all_to_all | solution.py:336
  63.4 5.2 %collective-permute-start.6 = (bf16[136,128]{1,0:T(8,128)(2,1)S(1)}, bf16[136,128]{1,0:T(8,128)(2,1)S(1)}, u32[]{:S(2)}, u32[]{:S(2)}) collective-permute-start(bf16[136,128]{1,0:T(8,128)(2,1)S(1)} %get-tuple-element.36.own), channel_id=1, source_target_pairs={{0,64},{64,0},{1,65},{65,1},{2,66},{66,2},{3,67},{67,3},{4,68},{68... | collective-permute-start | bytes 104456 | tf_op jit(solution)/shard_map/ppermute | solution.py:337
  68.6 0.9 collective-permute-done.6.core
  69.4 5.2 %collective-permute-start.7 = (bf16[200,128]{1,0:T(8,128)(2,1)S(1)}, bf16[200,128]{1,0:T(8,128)(2,1)S(1)}, u32[]{:S(2)}, u32[]{:S(2)}) collective-permute-start(bf16[200,128]{1,0:T(8,128)(2,1)S(1)} %pair.1.own), channel_id=1, source_target_pairs={{0,128},{128,0},{1,129},{129,1},{2,130},{130,2},{3,131},{131,3},{4... | collective-permute-start | bytes 153608 | tf_op jit(solution)/shard_map/ppermute | solution.py:339
  74.6 1.9 %collective-permute-done.7.zhi = bf16[200,128]{1,0:T(8,128)(2,1)S(1)} collective-permute-done((bf16[200,128]{1,0:T(8,128)(2,1)S(1)}, bf16[200,128]{1,0:T(8,128)(2,1)S(1)}, u32[]{:S(2)}, u32[]{:S(2)}) %collective-permute-start.7) | collective-permute-done | bytes 51232 | tf_op jit(solution)/shard_map/ppermute | solution.py:339
  76.5 0.7 join.1
  77.3 0.0 all-to-all-done.2.message_ref
  77.3 0.0 copy-start.4
  77.3 6.9 %all-to-all-start.3 = ((bf16[16,64,128]{2,1,0:T(8,128)(2,1)}), bf16[16,64,128]{2,1,0:T(8,128)(2,1)S(1)}, u32[]{:S(2)}, u32[]{:S(2)}) async-start(bf16[16,64,128]{2,1,0:T(8,128)(2,1)} %get-tuple-element.41), calls=%async_computation.3 | async-start | bytes 524288 | tf_op jit(solution)/shard_map/all_to_all | solution.py:346
  84.1 1.3 %convolution_bitcast_fusion = f32[16,128,128]{2,1,0:T(8,128)} fusion(bf16[4,2,1,16,128]{4,3,2,1,0:T(8,128)(2,1)S(1)} %get-tuple-element.46, bf16[4,2,1,16,128]{4,3,2,1,0:T(8,128)(2,1)S(1)} %get-tuple-element.45), kind=kOutput, calls=%fused_computation | convolution fusion | flops 4194304 | bytes 1114112 | tf_op jit(solution)/shard_map/gskc,gskd->kcd/dot_general | solution.py:353
  85.5 0.0 copy-done.4
  85.5 6.4 %finish.1 = bf16[2,4096,128]{2,1,0:T(8,128)(2,1)} custom-call(bf16[4096,1024]{1,0:T(8,128)(2,1)} %basis_ref.1, bf16[16,128,128]{2,1,0:T(8,128)(2,1)} %copy-done.4, bf16[2,4096,128]{2,1,0:T(8,128)(2,1)} %bitcast.19), custom_call_target="tpu_custom_call" | custom-call | flops 2147483648 | bytes 16777216 | tf_op jit(solution)/shard_map/finish/pallas_call | solution.py:275
  91.9 0.0 all-to-all-done.3.message
  91.9 0.8 weights.3
  (2 shorter events, 0.0 us)
Async XLA Ops:
  8.3 7.8 %copy-start.1 = (bf16[128,512]{1,0:T(8,128)(2,1)S(1)}, bf16[128,512]{1,0:T(8,128)(2,1)}, u32[]{:S(2)}) copy-start(bf16[128,512]{1,0:T(8,128)(2,1)} %up_ref.1) | copy-start | bytes 393220
  8.4 7.8 %copy-start.2 = (bf16[512,128]{1,0:T(8,128)(2,1)S(1)}, bf16[512,128]{1,0:T(8,128)(2,1)}, u32[]{:S(2)}) copy-start(bf16[512,128]{1,0:T(8,128)(2,1)} %down_ref.1) | copy-start | bytes 393220
  8.4 7.8 %copy-start.3 = (f32[512]{0:T(512)S(1)}, f32[512]{0:T(512)}, u32[]{:S(2)}) copy-start(f32[512]{0:T(512)} %param.12) | copy-start | bytes 6148
  8.4 25.4 %all-to-all-start = ((bf16[16,64,512]{2,1,0:T(8,128)(2,1)}), bf16[16,64,512]{2,1,0:T(8,128)(2,1)S(1)}, u32[]{:S(2)}, u32[]{:S(2)}) async-start(bf16[16,64,512]{2,1,0:T(8,128)(2,1)} %project.1), calls=%async_computation | async-start | bytes 2097152 | tf_op jit(solution)/shard_map/all_to_all | solution.py:316
  16.1 33.0 %copy-start = (bf16[16,128,128]{2,1,0:T(8,128)(2,1)S(1)}, bf16[16,128,128]{2,1,0:T(8,128)(2,1)}, u32[]{:S(2)}) copy-start(bf16[16,128,128]{2,1,0:T(8,128)(2,1)} %weights.2) | copy-start | bytes 1572868
  33.8 14.2 %all-to-all-start.1 = ((bf16[16,72,128]{2,1,0:T(8,128)(2,1)}), bf16[16,72,128]{2,1,0:T(8,128)(2,1)S(1)}, u32[]{:S(2)}, u32[]{:S(2)}) async-start(bf16[16,72,128]{2,1,0:T(8,128)(2,1)} %get-tuple-element.32), calls=%async_computation.1 | async-start | bytes 589824 | tf_op jit(solution)/shard_map/all_to_all | solution.py:321
  40.7 7.4 %collective-permute-start = (f32[16,512]{1,0:T(8,128)S(1)}, f32[16,512]{1,0:T(8,128)S(1)}, u32[]{:S(2)}, u32[]{:S(2)}) collective-permute-start(f32[16,512]{1,0:T(8,128)S(1)} %get-tuple-element.27), channel_id=1, source_target_pairs={{0,4},{4,8},{8,12},{12,0},{1,5},{5,9},{9,13},{13,1},{2,6},{6,10},{... | collective-permute-start | bytes 98312 | tf_op jit(solution)/shard_map/ppermute | solution.py:305
  42.4 5.7 %collective-permute-start.1 = (f32[16,512]{1,0:T(8,128)S(1)}, f32[16,512]{1,0:T(8,128)S(1)}, u32[]{:S(2)}, u32[]{:S(2)}) collective-permute-start(f32[16,512]{1,0:T(8,128)S(1)} %get-tuple-element.28), channel_id=1, source_target_pairs={{0,8},{4,12},{8,0},{12,4},{1,9},{5,13},{9,1},{13,5},{2,10},{6,14},... | collective-permute-start | bytes 98312 | tf_op jit(solution)/shard_map/ppermute | solution.py:305
  45.4 3.7 %collective-permute-start.2 = (f32[16,512]{1,0:T(8,128)S(1)}, f32[16,512]{1,0:T(8,128)S(1)}, u32[]{:S(2)}, u32[]{:S(2)}) collective-permute-start(f32[16,512]{1,0:T(8,128)S(1)} %get-tuple-element.29), channel_id=1, source_target_pairs={{0,12},{4,0},{8,4},{12,8},{1,13},{5,1},{9,5},{13,9},{2,14},{6,2},{... | collective-permute-start | bytes 98312 | tf_op jit(solution)/shard_map/ppermute | solution.py:305
  49.6 4.3 %collective-permute-start.5 = (bf16[104,128]{1,0:T(8,128)(2,1)S(1)}, bf16[104,128]{1,0:T(8,128)(2,1)S(1)}, u32[]{:S(2)}, u32[]{:S(2)}) collective-permute-start(bf16[104,128]{1,0:T(8,128)(2,1)S(1)} %get-tuple-element.33.own), channel_id=1, source_target_pairs={{0,12},{4,0},{8,4},{12,8},{1,13},{5,1},{9,5},{13,9},{2,14},{6,2},{... | collective-permute-start | bytes 79880 | tf_op jit(solution)/shard_map/ppermute | solution.py:305
  53.0 3.6 %collective-permute-start.4 = (bf16[104,128]{1,0:T(8,128)(2,1)S(1)}, bf16[104,128]{1,0:T(8,128)(2,1)S(1)}, u32[]{:S(2)}, u32[]{:S(2)}) collective-permute-start(bf16[104,128]{1,0:T(8,128)(2,1)S(1)} %get-tuple-element.33.own), channel_id=1, source_target_pairs={{0,8},{4,12},{8,0},{12,4},{1,9},{5,13},{9,1},{13,5},{2,10},{6,14},... | collective-permute-start | bytes 79880 | tf_op jit(solution)/shard_map/ppermute | solution.py:305
  53.0 4.8 %collective-permute-start.3 = (bf16[104,128]{1,0:T(8,128)(2,1)S(1)}, bf16[104,128]{1,0:T(8,128)(2,1)S(1)}, u32[]{:S(2)}, u32[]{:S(2)}) collective-permute-start(bf16[104,128]{1,0:T(8,128)(2,1)S(1)} %get-tuple-element.33.own), channel_id=1, source_target_pairs={{0,4},{4,8},{8,12},{12,0},{1,5},{5,9},{9,13},{13,1},{2,6},{6,10},{... | collective-permute-start | bytes 79880 | tf_op jit(solution)/shard_map/ppermute | solution.py:305
  58.6 18.6 %all-to-all-start.2 = ((bf16[16,128,128]{2,1,0:T(8,128)(2,1)}), bf16[16,128,128]{2,1,0:T(8,128)(2,1)S(1)}, u32[]{:S(2)}, u32[]{:S(2)}) async-start(bf16[16,128,128]{2,1,0:T(8,128)(2,1)} %get-tuple-element.35), calls=%async_computation.2 | async-start | bytes 1048576 | tf_op jit(solution)/shard_map/all_to_all | solution.py:336
  63.4 6.0 %collective-permute-start.6 = (bf16[136,128]{1,0:T(8,128)(2,1)S(1)}, bf16[136,128]{1,0:T(8,128)(2,1)S(1)}, u32[]{:S(2)}, u32[]{:S(2)}) collective-permute-start(bf16[136,128]{1,0:T(8,128)(2,1)S(1)} %get-tuple-element.36.own), channel_id=1, source_target_pairs={{0,64},{64,0},{1,65},{65,1},{2,66},{66,2},{3,67},{67,3},{4,68},{68... | collective-permute-start | bytes 104456 | tf_op jit(solution)/shard_map/ppermute | solution.py:337
  69.4 7.1 %collective-permute-start.7 = (bf16[200,128]{1,0:T(8,128)(2,1)S(1)}, bf16[200,128]{1,0:T(8,128)(2,1)S(1)}, u32[]{:S(2)}, u32[]{:S(2)}) collective-permute-start(bf16[200,128]{1,0:T(8,128)(2,1)S(1)} %pair.1.own), channel_id=1, source_target_pairs={{0,128},{128,0},{1,129},{129,1},{2,130},{130,2},{3,131},{131,3},{4... | collective-permute-start | bytes 153608 | tf_op jit(solution)/shard_map/ppermute | solution.py:339
  77.3 8.2 %copy-start.4 = (bf16[16,128,128]{2,1,0:T(8,128)(2,1)}, bf16[16,128,128]{2,1,0:T(8,128)(2,1)S(1)}, u32[]{:S(2)}) copy-start(bf16[16,128,128]{2,1,0:T(8,128)(2,1)S(1)} %all-to-all-done.2.message_ref) | copy-start | bytes 1572868
  77.3 14.6 %all-to-all-start.3 = ((bf16[16,64,128]{2,1,0:T(8,128)(2,1)}), bf16[16,64,128]{2,1,0:T(8,128)(2,1)S(1)}, u32[]{:S(2)}, u32[]{:S(2)}) async-start(bf16[16,64,128]{2,1,0:T(8,128)(2,1)} %get-tuple-element.41), calls=%async_computation.3 | async-start | bytes 524288 | tf_op jit(solution)/shard_map/all_to_all | solution.py:346

commit v6 on v5

--- a/solution.py
+++ b/solution.py
@@ -194,11 +194,11 @@
     total[...] = sums
     for shift, out in enumerate((own, one, two, three)):
         first = pl.multiple_of(lax.rem(z_at[0] + shift, RING) * 16, 16)
-        out[...] = total[pl.ds(first, 16), :]
+        out[...] = total[pl.ds(first, 16), :].astype(out.dtype)
 
 
 def own_body(own, one, two, three, weights, pieces, modes_ref, line_ref):
-    total = (own[...] + two[...]) + (one[...] + three[...])
+    total = (own[...] + two[...].astype(F32)) + (one[...].astype(F32) + three[...].astype(F32))
     for g in range(4):
         modes_ref[g * 16 : (g + 1) * 16, :] = total[:, g * 128 : (g + 1) * 128].astype(BF16)
     grads = pieces[0].astype(F32)
@@ -320,7 +320,7 @@
     torus = ("x", "y")
     pieces = lax.all_to_all(pieces, torus, 0, 0)
     own, *chunks = small(
-        line_body, "line", [struct((16, 512), F32)] * 4,
+        line_body, "line", [struct((16, 512), F32)] + [struct((16, 512), BF16)] * 3,
         z_at, messages, scratch=[pltpu.VMEM((64, 512), F32)],
     )
     arrived = [shift(chunks[s - 1], "zlo", s) for s in (1, 2, 3)]

time: 93.8 us -> 93.6 us (level)
  no operation moved by 1% of the time
where the time goes in v6:
time: 93.6 us; the launch traced here: 92.5 us
  starting transfers between devices  46.2 us (49%)
  Pallas kernels  34.8 us (37%)
  waiting for transfers between devices  9.36 us (10%)
  matrix products  1.35 us (1%)
    pallas_call x1, Pallas kernels, pointwise(): pl.pallas_call(pointwise_body, in_specs=[HBM, HBM] + [VMEM] * 3, out_spec...  17.6 us
    ppermute x6, starting transfers between devices, shift(): lax.ppermute(value, axis, [(i, (i + by) % RING) for i in range(RING)])  9.86 us
    all_to_all x1, starting transfers between devices, per_device(): messages = lax.all_to_all(packed, ('x', 'y'), 0, 0)  7.73 us
    pallas_call x1, Pallas kernels, project(): pl.pallas_call(project_body, in_specs=[HBM] * 3, out_specs=VMEM, out_shap...  7.71 us
    all_to_all x1, starting transfers between devices, per_device(): message = lax.all_to_all(message, torus, 0, 0)  6.86 us
    all_to_all x1, starting transfers between devices, per_device(): pieces = lax.all_to_all(pieces, torus, 0, 0)  6.66 us
    pallas_call x1, Pallas kernels, finish(): pl.pallas_call(finish_body, grid=(vertices // rows,), in_specs=[pl.BlockS...  6.38 us
    ppermute x1, starting transfers between devices, per_device(): zhi = lax.ppermute(pair, 'zhi', [(0, 1), (1, 0)])  5.2 us
  transfers between devices with their start and end apart: 12, of which 7 were waited for; matrix products, arithmetic and copies ran while one was open for 1% of the time, Pallas kernels for 27%

profile of v6, /device:TPU:1, one launch (start us, length us, event | category | flops | bytes accessed | tf_op | source)
XLA Modules:
  0.0 92.5 jit_solution(13861225500998220763)
XLA Ops:
  0.6 7.7 %project.1 = bf16[16,64,512]{2,1,0:T(8,128)(2,1)} custom-call(bf16[4096,1024]{1,0:T(8,128)(2,1)} %basis_ref.1, bf16[2,4096,128]{2,1,0:T(8,128)(2,1)} %x_hbm.1, bf16[2,4096,128]{2,1,0:T(8,128)(2,1)} %c_hbm.1), custom_call_target="tpu_custom_call" | custom-call | flops 4294967296 | bytes 13631488 | tf_op jit(solution)/shard_map/project/pallas_call | solution.py:70
  8.3 0.0 copy-start.1
  8.4 0.0 copy-start.2
  8.4 0.0 copy-start.3
  8.4 7.7 %all-to-all-start = ((bf16[16,64,512]{2,1,0:T(8,128)(2,1)}), bf16[16,64,512]{2,1,0:T(8,128)(2,1)S(1)}, u32[]{:S(2)}, u32[]{:S(2)}) async-start(bf16[16,64,512]{2,1,0:T(8,128)(2,1)} %project.1), calls=%async_computation | async-start | bytes 2097152 | tf_op jit(solution)/shard_map/all_to_all | solution.py:316
  16.1 0.0 copy-done.1
  16.1 0.0 copy-done.2
  16.1 0.0 copy-done.3
  16.1 0.0 copy-start
  16.2 17.6 %pointwise.1 = (bf16[8192,128]{1,0:T(8,128)(2,1)}, bf16[16,72,128]{2,1,0:T(8,128)(2,1)}) custom-call(bf16[8192,128]{1,0:T(8,128)(2,1)} %bitcast.20, bf16[8192,128]{1,0:T(8,128)(2,1)} %bitcast.21, bf16[128,512]{1,0:T(8,128)(2,1)S(1)} %copy-done.1, f32[1,512]{1,0:T(1,128)S(1)} %bitcast.18, bf16[512,128]{1,0:T(8,128)(2,1)S(1)} %copy-done.2), custom_call_target="tpu_custom_call" | custom-call | flops 5368709120 | bytes 8388608 | tf_op jit(solution)/shard_map/pointwise/pallas_call | solution.py:156
  33.8 0.0 all-to-all-done.messages
  33.8 6.7 %all-to-all-start.1 = ((bf16[16,72,128]{2,1,0:T(8,128)(2,1)}), bf16[16,72,128]{2,1,0:T(8,128)(2,1)S(1)}, u32[]{:S(2)}, u32[]{:S(2)}) async-start(bf16[16,72,128]{2,1,0:T(8,128)(2,1)} %get-tuple-element.32), calls=%async_computation.1 | async-start | bytes 589824 | tf_op jit(solution)/shard_map/all_to_all | solution.py:321
  40.5 0.2 line.1
  40.7 1.7 %collective-permute-start = (bf16[16,512]{1,0:T(8,128)(2,1)S(1)}, bf16[16,512]{1,0:T(8,128)(2,1)S(1)}, u32[]{:S(2)}, u32[]{:S(2)}) collective-permute-start(bf16[16,512]{1,0:T(8,128)(2,1)S(1)} %get-tuple-element.27), channel_id=1, source_target_pairs={{0,4},{4,8},{8,12},{12,0},{1,5},{5,9},{9,13},{13,1},{2,6},{6,10},{... | collective-permute-start | bytes 49160 | tf_op jit(solution)/shard_map/ppermute | solution.py:305
  42.4 3.0 %collective-permute-start.1 = (bf16[16,512]{1,0:T(8,128)(2,1)S(1)}, bf16[16,512]{1,0:T(8,128)(2,1)S(1)}, u32[]{:S(2)}, u32[]{:S(2)}) collective-permute-start(bf16[16,512]{1,0:T(8,128)(2,1)S(1)} %get-tuple-element.28), channel_id=1, source_target_pairs={{0,8},{4,12},{8,0},{12,4},{1,9},{5,13},{9,1},{13,5},{2,10},{6,14},... | collective-permute-start | bytes 49160 | tf_op jit(solution)/shard_map/ppermute | solution.py:305
  45.4 0.7 collective-permute-start.2
  46.1 2.0 %all-to-all-done.1.pieces = bf16[16,72,128]{2,1,0:T(8,128)(2,1)S(1)} async-done(((bf16[16,72,128]{2,1,0:T(8,128)(2,1)}), bf16[16,72,128]{2,1,0:T(8,128)(2,1)S(1)}, u32[]{:S(2)}, u32[]{:S(2)}) %all-to-all-start.1) | async-done | bytes 294944 | tf_op jit(solution)/shard_map/all_to_all | solution.py:321
  48.0 0.0 collective-permute-done.one
  48.1 0.0 collective-permute-done.1.two
  48.1 0.4 collective-permute-done.2.three
  48.4 0.0 copy-done
  48.4 0.5 own.1
  48.9 4.1 %collective-permute-start.5 = (bf16[104,128]{1,0:T(8,128)(2,1)S(1)}, bf16[104,128]{1,0:T(8,128)(2,1)S(1)}, u32[]{:S(2)}, u32[]{:S(2)}) collective-permute-start(bf16[104,128]{1,0:T(8,128)(2,1)S(1)} %get-tuple-element.33.own), channel_id=1, source_target_pairs={{0,12},{4,0},{8,4},{12,8},{1,13},{5,1},{9,5},{13,9},{2,14},{6,2},{... | collective-permute-start | bytes 79880 | tf_op jit(solution)/shard_map/ppermute | solution.py:305
  53.0 0.0 collective-permute-start.4
  53.0 0.4 collective-permute-start.3
  53.4 0.6 collective-permute-done.5.three
  53.9 2.6 %collective-permute-done.4.two = bf16[104,128]{1,0:T(8,128)(2,1)S(1)} collective-permute-done((bf16[104,128]{1,0:T(8,128)(2,1)S(1)}, bf16[104,128]{1,0:T(8,128)(2,1)S(1)}, u32[]{:S(2)}, u32[]{:S(2)}) %collective-permute-start.4) | collective-permute-done | bytes 26656 | tf_op jit(solution)/shard_map/ppermute | solution.py:305
  56.6 1.1 %collective-permute-done.3.one = bf16[104,128]{1,0:T(8,128)(2,1)S(1)} collective-permute-done((bf16[104,128]{1,0:T(8,128)(2,1)S(1)}, bf16[104,128]{1,0:T(8,128)(2,1)S(1)}, u32[]{:S(2)}, u32[]{:S(2)}) %collective-permute-start.3) | collective-permute-done | bytes 26656 | tf_op jit(solution)/shard_map/ppermute | solution.py:305
  57.7 0.9 gather.1
  58.5 4.7 %all-to-all-start.2 = ((bf16[16,128,128]{2,1,0:T(8,128)(2,1)}), bf16[16,128,128]{2,1,0:T(8,128)(2,1)S(1)}, u32[]{:S(2)}, u32[]{:S(2)}) async-start(bf16[16,128,128]{2,1,0:T(8,128)(2,1)} %get-tuple-element.35), calls=%async_computation.2 | async-start | bytes 1048576 | tf_op jit(solution)/shard_map/all_to_all | solution.py:336
  63.2 5.2 %collective-permute-start.6 = (bf16[136,128]{1,0:T(8,128)(2,1)S(1)}, bf16[136,128]{1,0:T(8,128)(2,1)S(1)}, u32[]{:S(2)}, u32[]{:S(2)}) collective-permute-start(bf16[136,128]{1,0:T(8,128)(2,1)S(1)} %get-tuple-element.36.own), channel_id=1, source_target_pairs={{0,64},{64,0},{1,65},{65,1},{2,66},{66,2},{3,67},{67,3},{4,68},{68... | collective-permute-start | bytes 104456 | tf_op jit(solution)/shard_map/ppermute | solution.py:337
  68.4 0.9 collective-permute-done.6.core
  69.3 5.2 %collective-permute-start.7 = (bf16[200,128]{1,0:T(8,128)(2,1)S(1)}, bf16[200,128]{1,0:T(8,128)(2,1)S(1)}, u32[]{:S(2)}, u32[]{:S(2)}) collective-permute-start(bf16[200,128]{1,0:T(8,128)(2,1)S(1)} %pair.1.own), channel_id=1, source_target_pairs={{0,128},{128,0},{1,129},{129,1},{2,130},{130,2},{3,131},{131,3},{4... | collective-permute-start | bytes 153608 | tf_op jit(solution)/shard_map/ppermute | solution.py:339
  74.5 1.9 %collective-permute-done.7.zhi = bf16[200,128]{1,0:T(8,128)(2,1)S(1)} collective-permute-done((bf16[200,128]{1,0:T(8,128)(2,1)S(1)}, bf16[200,128]{1,0:T(8,128)(2,1)S(1)}, u32[]{:S(2)}, u32[]{:S(2)}) %collective-permute-start.7) | collective-permute-done | bytes 51232 | tf_op jit(solution)/shard_map/ppermute | solution.py:339
  76.3 0.7 join.1
  77.1 0.0 all-to-all-done.2.message_ref
  77.1 0.0 copy-start.4
  77.1 6.9 %all-to-all-start.3 = ((bf16[16,64,128]{2,1,0:T(8,128)(2,1)}), bf16[16,64,128]{2,1,0:T(8,128)(2,1)S(1)}, u32[]{:S(2)}, u32[]{:S(2)}) async-start(bf16[16,64,128]{2,1,0:T(8,128)(2,1)} %get-tuple-element.41), calls=%async_computation.3 | async-start | bytes 524288 | tf_op jit(solution)/shard_map/all_to_all | solution.py:346
  84.0 1.3 %convolution_bitcast_fusion = f32[16,128,128]{2,1,0:T(8,128)} fusion(bf16[4,2,1,16,128]{4,3,2,1,0:T(8,128)(2,1)S(1)} %get-tuple-element.46, bf16[4,2,1,16,128]{4,3,2,1,0:T(8,128)(2,1)S(1)} %get-tuple-element.45), kind=kOutput, calls=%fused_computation | convolution fusion | flops 4194304 | bytes 1114112 | tf_op jit(solution)/shard_map/gskc,gskd->kcd/dot_general | solution.py:353
  85.3 0.0 copy-done.4
  85.3 6.4 %finish.1 = bf16[2,4096,128]{2,1,0:T(8,128)(2,1)} custom-call(bf16[4096,1024]{1,0:T(8,128)(2,1)} %basis_ref.1, bf16[16,128,128]{2,1,0:T(8,128)(2,1)} %copy-done.4, bf16[2,4096,128]{2,1,0:T(8,128)(2,1)} %bitcast.19), custom_call_target="tpu_custom_call" | custom-call | flops 2147483648 | bytes 16777216 | tf_op jit(solution)/shard_map/finish/pallas_call | solution.py:275
  91.7 0.0 all-to-all-done.3.message
  91.7 0.8 weights.3
  (2 shorter events, 0.0 us)
Async XLA Ops:
  8.3 7.8 %copy-start.1 = (bf16[128,512]{1,0:T(8,128)(2,1)S(1)}, bf16[128,512]{1,0:T(8,128)(2,1)}, u32[]{:S(2)}) copy-start(bf16[128,512]{1,0:T(8,128)(2,1)} %up_ref.1) | copy-start | bytes 393220
  8.4 7.8 %copy-start.2 = (bf16[512,128]{1,0:T(8,128)(2,1)S(1)}, bf16[512,128]{1,0:T(8,128)(2,1)}, u32[]{:S(2)}) copy-start(bf16[512,128]{1,0:T(8,128)(2,1)} %down_ref.1) | copy-start | bytes 393220
  8.4 7.8 %copy-start.3 = (f32[512]{0:T(512)S(1)}, f32[512]{0:T(512)}, u32[]{:S(2)}) copy-start(f32[512]{0:T(512)} %param.12) | copy-start | bytes 6148
  8.4 25.4 %all-to-all-start = ((bf16[16,64,512]{2,1,0:T(8,128)(2,1)}), bf16[16,64,512]{2,1,0:T(8,128)(2,1)S(1)}, u32[]{:S(2)}, u32[]{:S(2)}) async-start(bf16[16,64,512]{2,1,0:T(8,128)(2,1)} %project.1), calls=%async_computation | async-start | bytes 2097152 | tf_op jit(solution)/shard_map/all_to_all | solution.py:316
  16.1 32.3 %copy-start = (bf16[16,128,128]{2,1,0:T(8,128)(2,1)S(1)}, bf16[16,128,128]{2,1,0:T(8,128)(2,1)}, u32[]{:S(2)}) copy-start(bf16[16,128,128]{2,1,0:T(8,128)(2,1)} %weights.2) | copy-start | bytes 1572868
  33.8 14.2 %all-to-all-start.1 = ((bf16[16,72,128]{2,1,0:T(8,128)(2,1)}), bf16[16,72,128]{2,1,0:T(8,128)(2,1)S(1)}, u32[]{:S(2)}, u32[]{:S(2)}) async-start(bf16[16,72,128]{2,1,0:T(8,128)(2,1)} %get-tuple-element.32), calls=%async_computation.1 | async-start | bytes 589824 | tf_op jit(solution)/shard_map/all_to_all | solution.py:321
  40.7 7.4 %collective-permute-start = (bf16[16,512]{1,0:T(8,128)(2,1)S(1)}, bf16[16,512]{1,0:T(8,128)(2,1)S(1)}, u32[]{:S(2)}, u32[]{:S(2)}) collective-permute-start(bf16[16,512]{1,0:T(8,128)(2,1)S(1)} %get-tuple-element.27), channel_id=1, source_target_pairs={{0,4},{4,8},{8,12},{12,0},{1,5},{5,9},{9,13},{13,1},{2,6},{6,10},{... | collective-permute-start | bytes 49160 | tf_op jit(solution)/shard_map/ppermute | solution.py:305
  42.4 5.7 %collective-permute-start.1 = (bf16[16,512]{1,0:T(8,128)(2,1)S(1)}, bf16[16,512]{1,0:T(8,128)(2,1)S(1)}, u32[]{:S(2)}, u32[]{:S(2)}) collective-permute-start(bf16[16,512]{1,0:T(8,128)(2,1)S(1)} %get-tuple-element.28), channel_id=1, source_target_pairs={{0,8},{4,12},{8,0},{12,4},{1,9},{5,13},{9,1},{13,5},{2,10},{6,14},... | collective-permute-start | bytes 49160 | tf_op jit(solution)/shard_map/ppermute | solution.py:305
  45.4 3.0 %collective-permute-start.2 = (bf16[16,512]{1,0:T(8,128)(2,1)S(1)}, bf16[16,512]{1,0:T(8,128)(2,1)S(1)}, u32[]{:S(2)}, u32[]{:S(2)}) collective-permute-start(bf16[16,512]{1,0:T(8,128)(2,1)S(1)} %get-tuple-element.29), channel_id=1, source_target_pairs={{0,12},{4,0},{8,4},{12,8},{1,13},{5,1},{9,5},{13,9},{2,14},{6,2},{... | collective-permute-start | bytes 49160 | tf_op jit(solution)/shard_map/ppermute | solution.py:305
  48.9 5.0 %collective-permute-start.5 = (bf16[104,128]{1,0:T(8,128)(2,1)S(1)}, bf16[104,128]{1,0:T(8,128)(2,1)S(1)}, u32[]{:S(2)}, u32[]{:S(2)}) collective-permute-start(bf16[104,128]{1,0:T(8,128)(2,1)S(1)} %get-tuple-element.33.own), channel_id=1, source_target_pairs={{0,12},{4,0},{8,4},{12,8},{1,13},{5,1},{9,5},{13,9},{2,14},{6,2},{... | collective-permute-start | bytes 79880 | tf_op jit(solution)/shard_map/ppermute | solution.py:305
  53.0 3.6 %collective-permute-start.4 = (bf16[104,128]{1,0:T(8,128)(2,1)S(1)}, bf16[104,128]{1,0:T(8,128)(2,1)S(1)}, u32[]{:S(2)}, u32[]{:S(2)}) collective-permute-start(bf16[104,128]{1,0:T(8,128)(2,1)S(1)} %get-tuple-element.33.own), channel_id=1, source_target_pairs={{0,8},{4,12},{8,0},{12,4},{1,9},{5,13},{9,1},{13,5},{2,10},{6,14},... | collective-permute-start | bytes 79880 | tf_op jit(solution)/shard_map/ppermute | solution.py:305
  53.0 4.7 %collective-permute-start.3 = (bf16[104,128]{1,0:T(8,128)(2,1)S(1)}, bf16[104,128]{1,0:T(8,128)(2,1)S(1)}, u32[]{:S(2)}, u32[]{:S(2)}) collective-permute-start(bf16[104,128]{1,0:T(8,128)(2,1)S(1)} %get-tuple-element.33.own), channel_id=1, source_target_pairs={{0,4},{4,8},{8,12},{12,0},{1,5},{5,9},{9,13},{13,1},{2,6},{6,10},{... | collective-permute-start | bytes 79880 | tf_op jit(solution)/shard_map/ppermute | solution.py:305
  58.5 18.5 %all-to-all-start.2 = ((bf16[16,128,128]{2,1,0:T(8,128)(2,1)}), bf16[16,128,128]{2,1,0:T(8,128)(2,1)S(1)}, u32[]{:S(2)}, u32[]{:S(2)}) async-start(bf16[16,128,128]{2,1,0:T(8,128)(2,1)} %get-tuple-element.35), calls=%async_computation.2 | async-start | bytes 1048576 | tf_op jit(solution)/shard_map/all_to_all | solution.py:336
  63.2 6.0 %collective-permute-start.6 = (bf16[136,128]{1,0:T(8,128)(2,1)S(1)}, bf16[136,128]{1,0:T(8,128)(2,1)S(1)}, u32[]{:S(2)}, u32[]{:S(2)}) collective-permute-start(bf16[136,128]{1,0:T(8,128)(2,1)S(1)} %get-tuple-element.36.own), channel_id=1, source_target_pairs={{0,64},{64,0},{1,65},{65,1},{2,66},{66,2},{3,67},{67,3},{4,68},{68... | collective-permute-start | bytes 104456 | tf_op jit(solution)/shard_map/ppermute | solution.py:337
  69.3 7.1 %collective-permute-start.7 = (bf16[200,128]{1,0:T(8,128)(2,1)S(1)}, bf16[200,128]{1,0:T(8,128)(2,1)S(1)}, u32[]{:S(2)}, u32[]{:S(2)}) collective-permute-start(bf16[200,128]{1,0:T(8,128)(2,1)S(1)} %pair.1.own), channel_id=1, source_target_pairs={{0,128},{128,0},{1,129},{129,1},{2,130},{130,2},{3,131},{131,3},{4... | collective-permute-start | bytes 153608 | tf_op jit(solution)/shard_map/ppermute | solution.py:339
  77.1 8.2 %copy-start.4 = (bf16[16,128,128]{2,1,0:T(8,128)(2,1)}, bf16[16,128,128]{2,1,0:T(8,128)(2,1)S(1)}, u32[]{:S(2)}) copy-start(bf16[16,128,128]{2,1,0:T(8,128)(2,1)S(1)} %all-to-all-done.2.message_ref) | copy-start | bytes 1572868
  77.1 14.6 %all-to-all-start.3 = ((bf16[16,64,128]{2,1,0:T(8,128)(2,1)}), bf16[16,64,128]{2,1,0:T(8,128)(2,1)S(1)}, u32[]{:S(2)}, u32[]{:S(2)}) async-start(bf16[16,64,128]{2,1,0:T(8,128)(2,1)} %get-tuple-element.41), calls=%async_computation.3 | async-start | bytes 524288 | tf_op jit(solution)/shard_map/all_to_all | solution.py:346
